TPU v7x, 128 devices: a whole 4x4x4 slice. The times are simulated.
128 devices in a mesh: cells: 8 (over y, z_lo), sensors: 16 (over z_hi, x, core).
Axes of the slice: x: 4, y: 4, z: 4 (z_hi: 2, z_lo: 2; z = z_hi * 2 + z_lo), core: 2. Of those that a mesh axis runs over, the one named last changes fastest.
Arguments:
- rhs: float32 [256, 6, 128, 128], P('sensors', None, 'cells'), may hold values from -18 to 18
- forward_map: bfloat16 [2, 128, 128, 16384], P(None, None, 'sensors', 'cells'), may hold values from -0.125 to 0.125
- stiffness: float32 [128, 128], P('cells'), may hold values from 0.5 to 1.5
- reaction: float32 [128, 128], P('cells'), may hold values from 0.25 to 2
- noise_weight: float32 [128], replicated, may hold values from 0.3 to 3
- sensor_cell: int32 [128], replicated, may hold values from 0 to 16383, as said below
Outputs:
- solution: float32 [256, 6, 128, 128], P('sensors', None, 'cells')
- residual: float32 [256, 6, 128, 128], P('sensors', None, 'cells')
Inputs may be any that keep to these rules, and one draw needn't show every extreme that they name: `sensor_cell`: row-major index over the 128 x 128 grid of the cell under each sensor; several sensors may share a cell.
All inputs are finite; a program needn't handle non-finite values.
Results may differ from a plain program's by a relative error of at most 0.0073.
Values may be sent and summed in bfloat16 or wider, within the bound.
A program may use at most 128 MiB of HBM per device.

v0:
```python
import math

import jax
import jax.numpy as jnp
from jax import lax
from jax.sharding import PartitionSpec as P

SWEEPS = 4
ITERS = 2


DAMPING = 0.8


def padded_2(array, sides, width):
    for axis, dim in sides:
        size, length = (lax.axis_size(axis), array.shape[dim])
        up = [(i, (i + 1) % size) for i in range(size - 1)]
        down = [(j, i) for i, j in up]
        last = lax.slice_in_dim(array, length - width, length, axis=dim)
        first = lax.slice_in_dim(array, 0, width, axis=dim)
        before = lax.ppermute(last, axis, up)
        after = lax.ppermute(first, axis, down)
        array = jnp.concatenate([before, array, after], axis=dim)
    return array


def neighbour_sum(extended):
    padded = jnp.pad(extended, [(0, 0)] * (extended.ndim - 1) + [(1, 1)])
    return (
        padded[..., 2:, 1:-1]
        + padded[..., :-2, 1:-1]
        + padded[..., 1:-1, 2:]
        + padded[..., 1:-1, :-2]
    )


def transform_table(freqs, period):
    wave = jnp.arange(freqs, dtype=jnp.int32)[:, None]
    moment = jnp.arange(period, dtype=jnp.int32)[None, :]
    phase = (wave * moment % period).astype(jnp.float32) * (2.0 * math.pi / period)
    factor = 1.0 / math.sqrt(period)
    return jnp.concatenate([jnp.cos(phase) * factor, -jnp.sin(phase) * factor], axis=0).astype(
        jnp.bfloat16
    )


def observe(map_pair, spectrum, sensor_marks):
    freqs = map_pair.shape[1]
    field_real = spectrum[:freqs]
    field_imag = spectrum[freqs:]

    def project(weights, values):
        return jnp.einsum("fsc,fbc->fbs", weights, values, preferred_element_type=jnp.float32)

    def select_cells(values):
        return jnp.einsum("fbc,cs->fbs", values, sensor_marks, preferred_element_type=jnp.float32)

    obs_real = (
        project(map_pair[0], field_real)
        - project(map_pair[1], field_imag)
        + select_cells(field_real)
    )
    obs_imag = (
        project(map_pair[0], field_imag)
        + project(map_pair[1], field_real)
        + select_cells(field_imag)
    )
    return jnp.stack([obs_real, obs_imag])


def pull_back(map_pair, weighted, sensor_marks):

    def spread_back(weights, values):
        return jnp.einsum("fsc,fbs->fbc", weights, values, preferred_element_type=jnp.float32)

    def place_cells(values):
        return jnp.einsum("fbs,cs->fbc", values, sensor_marks, preferred_element_type=jnp.float32)

    back_real = (
        spread_back(map_pair[0], weighted[0])
        + spread_back(map_pair[1], weighted[1])
        + place_cells(weighted[0])
    )
    back_imag = (
        spread_back(map_pair[0], weighted[1])
        - spread_back(map_pair[1], weighted[0])
        + place_cells(weighted[1])
    )
    return jnp.concatenate([back_real, back_imag], axis=0)


def shards(rhs, forward_map, stiffness, reaction, noise_weight, sensor_cell):
    time_here, samples, rows_here, grid_cols = rhs.shape
    freqs = forward_map.shape[1]
    period = 2 * freqs
    depth = SWEEPS - 1
    table = transform_table(freqs, period)
    table_wide = table.astype(jnp.float32)
    diagonal = reaction + 4.0 * stiffness * stiffness
    inverse = 1.0 / diagonal
    stiff_rim = padded_2(stiffness, (("cells", 0),), 1)

    def precondition(residual):
        update = DAMPING * inverse * residual
        for sweep in range(depth):
            update_wide = padded_2(update, (("cells", 2),), 1)
            applied = diagonal * update - stiffness * neighbour_sum(stiff_rim * update_wide)
            update = update + DAMPING * inverse * (residual - applied)
        return update

    cell_index = lax.axis_index("cells")
    sensor_index = lax.axis_index("sensors")
    cells_here = rows_here * grid_cols
    sensors_here = forward_map.shape[2]
    local_sensors = lax.dynamic_slice_in_dim(sensor_cell, sensor_index * sensors_here, sensors_here)
    cell_ids = cell_index * cells_here + jnp.arange(cells_here, dtype=jnp.int32)
    sensor_marks = (cell_ids[:, None] == local_sensors[None, :]).astype(jnp.bfloat16)
    local_weight = lax.dynamic_slice_in_dim(noise_weight, sensor_index * sensors_here, sensors_here)
    solution = precondition(rhs)
    residual = rhs
    for iteration in range(ITERS):
        field_wide = padded_2(solution.astype(jnp.bfloat16), (("cells", 2),), 1).astype(
            solution.dtype
        )
        prior_part = diagonal * solution - stiffness * neighbour_sum(stiff_rim * field_wide)
        field_low = solution.astype(jnp.bfloat16).reshape(time_here, samples, cells_here)
        spectrum = jnp.einsum(
            "jt,tbc->jbc",
            table,
            lax.all_gather(field_low, "sensors", axis=0, tiled=True),
            preferred_element_type=jnp.float32,
        ).astype(jnp.bfloat16)
        observed = lax.psum(observe(forward_map, spectrum, sensor_marks), "cells")
        weighted = (local_weight * observed).astype(jnp.bfloat16)
        adjoint = pull_back(forward_map, weighted, sensor_marks)
        result = lax.psum_scatter(
            jnp.einsum(
                "jt,jbc->tbc",
                table_wide,
                adjoint,
                precision=lax.Precision.HIGHEST,
                preferred_element_type=jnp.float32,
            ),
            "sensors",
            scatter_dimension=0,
            tiled=True,
        )
        residual = rhs - (prior_part + result.reshape(solution.shape))
        solution = solution + precondition(residual)
    return (solution, residual)


def solution(mesh):
    placed = (
        P("sensors", None, "cells", None),
        P(None, None, "sensors", "cells"),
        P("cells", None),
        P("cells", None),
        P(),
        P(),
    )
    return jax.shard_map(
        shards,
        mesh=mesh,
        in_specs=placed,
        out_specs=(P("sensors", None, "cells", None), P("sensors", None, "cells", None)),
        check_vma=False,
    )
```

profile of v0, /device:TPU:0, one launch (start us, length us, event | category | flops | bytes accessed | tf_op | source)
XLA Modules:
  0.0 730.2 jit_solution(10475129787735325284)
XLA Ops:
  17.2 5.5 collective-permute-start.2
  27.2 5.4 collective-permute-start.4
  36.5 5.8 collective-permute-start.6
  46.8 69.5 %all-gather.3.cloned.1.call-done = bf16[256,6,2048]{2,0,1:T(8,128)(2,1)} async-done(((bf16[16,6,2048]{2,0,1:T(8,128)(2,1)}), bf16[256,6,2048]{2,0,1:T(8,128)(2,1)}) %all-gather.3.cloned.1.call-update) | async-done | bytes 6291472 | tf_op jit(solution)/shard_map/all_gather | solution.py:131
  138.7 6.5 fusion.107
  145.3 33.8 %psum.14 = f32[2,128,6,8]{1,3,2,0:T(8,128)S(1)} all-reduce(f32[2,128,6,8]{1,3,2,0:T(8,128)S(1)} %pad_maximum_fusion), channel_id=1, replica_groups=mesh['cells'=8,'sensors'=16] {'cells'}, use_global_device_ids=true, to_apply=%region_0.1 | all-reduce | flops 12288 | bytes 98304 | tf_op jit(solution)/shard_map/psum | solution.py:134
  179.4 6.7 fusion.46
  186.1 6.8 fusion.36
  193.1 6.9 fusion.34
  203.6 12.6 %fusion.10 = f32[128,6,2048]{2,0,1:T(8,128)S(1)} fusion(f32[128,6,2048]{2,1,0:T(8,128)} %fusion.34, f32[128,6,2048]{2,1,0:T(8,128)S(1)} %bitcast.142, s32[2048]{0:T(1024)S(1)} %iota_add_fusion, s32[8]{0:T(128)S(1)} %dynamic_slice.7, bf16[2,128,6,8]{1,3,2,0:T(8,128)(2,1)S(1)} %multiply_convert_fusion.3), kind=kOutput, calls=%fused_computation.13 | convolution fusion | flops 28327936 | bytes 20992512 | tf_op jit(solution)/shard_map/fbs,cs->fbc/dot_general | solution.py:78
  216.2 9.7 %fusion.11 = f32[128,6,2048]{2,0,1:T(8,128)} fusion(f32[128,6,2048]{2,1,0:T(8,128)S(1)} %bitcast.140, f32[128,6,2048]{2,1,0:T(8,128)S(1)} %fusion.48, s32[2048]{0:T(1024)S(1)} %iota_add_fusion, s32[8]{0:T(128)S(1)} %dynamic_slice.7, bf16[2,128,6,8]{1,3,2,0:T(8,128)(2,1)S(1)} %multiply_convert_fusion.3), kind=kOutput, calls=%fused_computation.15 | convolution fusion | flops 28327936 | bytes 23089664 | tf_op jit(solution)/shard_map/fbs,cs->fbc/dot_general | solution.py:78
  225.9 11.7 %fusion = f32[256,6,2048]{2,0,1:T(8,128)} fusion(f32[128,6,2048]{2,0,1:T(8,128)S(1)} %fusion.10, f32[128,6,2048]{2,0,1:T(8,128)} %fusion.11, bf16[128,256]{1,0:T(8,128)(2,1)S(1)} %get-tuple-element.44, bf16[128,256]{1,0:T(8,128)(2,1)S(1)} %get-tuple-element.45), kind=kOutput, calls=%fused_computation | convolution fusion | flops 9667084288 | bytes 25296896 | tf_op jit(solution)/shard_map/jt,jbc->tbc/dot_general | solution.py:138
  245.6 111.0 %reduce-scatter.3.cloned.1.call-done = f32[16,6,2048]{2,0,1:T(8,128)} async-done(((f32[256,6,2048]{2,0,1:T(8,128)}), f32[16,6,2048]{2,0,1:T(8,128)}) %reduce-scatter.3.cloned.1.call-update) | async-done | bytes 786448 | tf_op jit(solution)/shard_map/reduce_scatter | solution.py:137
  377.1 5.4 collective-permute-start.14
  387.4 67.0 %all-gather.5.cloned.1.call-done = bf16[256,6,2048]{2,0,1:T(8,128)(2,1)} async-done(((bf16[16,6,2048]{2,0,1:T(8,128)(2,1)}), bf16[256,6,2048]{2,0,1:T(8,128)(2,1)}) %all-gather.5.cloned.1.call-update) | async-done | bytes 6291472 | tf_op jit(solution)/shard_map/all_gather | solution.py:131
  476.3 6.2 fusion.87
  482.7 33.8 %psum.15 = f32[2,128,6,8]{1,3,2,0:T(8,128)S(1)} all-reduce(f32[2,128,6,8]{1,3,2,0:T(8,128)S(1)} %pad_maximum_fusion.1), channel_id=1, replica_groups=mesh['cells'=8,'sensors'=16] {'cells'}, use_global_device_ids=true, to_apply=%region_2.3 | all-reduce | flops 12288 | bytes 98304 | tf_op jit(solution)/shard_map/psum | solution.py:134
  516.8 6.7 fusion.40
  523.5 6.8 fusion.30
  530.4 6.9 fusion.28
  541.0 12.6 %fusion.8 = f32[128,6,2048]{2,0,1:T(8,128)S(1)} fusion(f32[128,6,2048]{2,1,0:T(8,128)} %fusion.28, f32[128,6,2048]{2,1,0:T(8,128)S(1)} %bitcast.144, s32[2048]{0:T(1024)S(1)} %iota_add_fusion, s32[8]{0:T(128)S(1)} %dynamic_slice.7, bf16[2,128,6,8]{1,3,2,0:T(8,128)(2,1)S(1)} %multiply_convert_fusion.2), kind=kOutput, calls=%fused_computation.9 | convolution fusion | flops 28327936 | bytes 20992512 | tf_op jit(solution)/shard_map/fbs,cs->fbc/dot_general | solution.py:78
  553.6 9.7 %fusion.9 = f32[128,6,2048]{2,0,1:T(8,128)} fusion(f32[128,6,2048]{2,1,0:T(8,128)S(1)} %bitcast.138, f32[128,6,2048]{2,1,0:T(8,128)S(1)} %fusion.42, s32[2048]{0:T(1024)S(1)} %iota_add_fusion, s32[8]{0:T(128)S(1)} %dynamic_slice.7, bf16[2,128,6,8]{1,3,2,0:T(8,128)(2,1)S(1)} %multiply_convert_fusion.2), kind=kOutput, calls=%fused_computation.11 | convolution fusion | flops 28327936 | bytes 23089664 | tf_op jit(solution)/shard_map/fbs,cs->fbc/dot_general | solution.py:78
  563.3 11.7 %fusion.4 = f32[256,6,2048]{2,0,1:T(8,128)} fusion(f32[128,6,2048]{2,0,1:T(8,128)S(1)} %fusion.8, f32[128,6,2048]{2,0,1:T(8,128)} %fusion.9, bf16[128,256]{1,0:T(8,128)(2,1)S(1)} %get-tuple-element.44, bf16[128,256]{1,0:T(8,128)(2,1)S(1)} %get-tuple-element.45), kind=kOutput, calls=%fused_computation.4 | convolution fusion | flops 9667084288 | bytes 25296896 | tf_op jit(solution)/shard_map/jt,jbc->tbc/dot_general | solution.py:138
  583.1 111.0 %reduce-scatter.5.cloned.1.call-done = f32[16,6,2048]{2,0,1:T(8,128)} async-done(((f32[256,6,2048]{2,0,1:T(8,128)}), f32[16,6,2048]{2,0,1:T(8,128)}) %reduce-scatter.5.cloned.1.call-update) | async-done | bytes 786448 | tf_op jit(solution)/shard_map/reduce_scatter | solution.py:137
  (175 shorter events, 145.9 us)
Async XLA Ops:
  7.2 109.1 %all-gather.3.cloned.1.call-start = ((), (), s32[]{:S(2)}) async-start(), calls=%async_computation.2 | async-start | bytes 6684672 | tf_op jit(solution)/shard_map/all_gather | solution.py:131
  8.0 14.6 %collective-permute-start.1 = (f32[1,128]{1,0:T(1,128)S(1)}, f32[1,128]{1,0:T(1,128)S(1)}, u32[]{:S(2)}, u32[]{:S(2)}) collective-permute-start(f32[1,128]{1,0:T(1,128)S(1)} %get-tuple-element.43), channel_id=1, source_target_pairs={{16,0},{32,16},{48,32},{64,48},{80,64},{96,80},{112,96},{17,1},{33... | collective-permute-start | bytes 1544 | tf_op jit(solution)/shard_map/ppermute | solution.py:23
  9.3 13.3 %collective-permute-start = (f32[1,128]{1,0:T(1,128)S(1)}, f32[1,128]{1,0:T(1,128)S(1)}, u32[]{:S(2)}, u32[]{:S(2)}) collective-permute-start(f32[1,128]{1,0:T(1,128)S(1)} %get-tuple-element.42), channel_id=1, source_target_pairs={{0,16},{16,32},{32,48},{48,64},{64,80},{80,96},{96,112},{1,17},{17... | collective-permute-start | bytes 1544 | tf_op jit(solution)/shard_map/ppermute | solution.py:22
  15.9 7.5 %collective-permute-start.3 = (f32[16,6,1,128]{3,2,1,0:T(1,128)S(1)}, f32[16,6,1,128]{3,2,1,0:T(1,128)S(1)}, u32[]{:S(2)}, u32[]{:S(2)}) collective-permute-start(f32[16,6,1,128]{3,2,1,0:T(1,128)S(1)} %get-tuple-element.33), channel_id=1, source_target_pairs={{16,0},{32,16},{48,32},{64,48},{80,64},{96,80},{112,96},{17,1},{33... | collective-permute-start | bytes 147464 | tf_op jit(solution)/shard_map/ppermute | solution.py:23
  17.2 7.2 collective-permute-start.2
  25.9 6.9 collective-permute-start.5
  27.2 7.2 collective-permute-start.4
  35.2 7.2 collective-permute-start.7
  36.5 7.5 %collective-permute-start.6 = (f32[16,6,1,128]{3,2,1,0:T(1,128)S(1)}, f32[16,6,1,128]{3,2,1,0:T(1,128)S(1)}, u32[]{:S(2)}, u32[]{:S(2)}) collective-permute-start(f32[16,6,1,128]{3,2,1,0:T(1,128)S(1)} %get-tuple-element.28), channel_id=1, source_target_pairs={{0,16},{16,32},{32,48},{48,64},{64,80},{80,96},{96,112},{1,17},{17... | collective-permute-start | bytes 147464 | tf_op jit(solution)/shard_map/ppermute | solution.py:22
  45.8 310.8 %reduce-scatter.3.cloned.1.call-start = ((), (), s32[]{:S(2)}) async-start(), calls=%async_computation.3 | async-start | bytes 13369344 | tf_op jit(solution)/shard_map/reduce_scatter | solution.py:137
  237.6 216.9 %all-gather.5.cloned.1.call-start = ((), (), s32[]{:S(2)}) async-start(), calls=%async_computation.4 | async-start | bytes 6684672 | tf_op jit(solution)/shard_map/all_gather | solution.py:131
  239.0 6.3 collective-permute-start.8
  359.8 6.3 collective-permute-start.10
  367.0 6.3 collective-permute-start.13
  368.3 6.6 collective-permute-start.12
  375.8 6.9 collective-permute-start.15
  377.1 7.2 collective-permute-start.14
  387.0 307.1 %reduce-scatter.5.cloned.1.call-start = ((), (), s32[]{:S(2)}) async-start(), calls=%async_computation.5 | async-start | bytes 13369344 | tf_op jit(solution)/shard_map/reduce_scatter | solution.py:137
  576.5 6.3 collective-permute-start.16
  697.3 6.3 collective-permute-start.18
  704.4 6.3 collective-permute-start.21
  705.7 6.6 collective-permute-start.20
  713.2 6.9 collective-permute-start.23
  714.5 7.2 collective-permute-start.22
  (22 other events, 310.4 us)
Sparse Core Ops, SparseCore 0:
  46.0 70.2 all-gather.2
  237.7 118.8 reduce-scatter.2
  387.1 67.2 all-gather.4
  575.1 118.9 reduce-scatter.4
where the time goes:
time: 739 us; the launch traced here: 730 us
  waiting for transfers between devices  377 us (51%)
  matrix products  166 us (22%)
  starting transfers between devices  76.7 us (10%)
  blocking collectives  67.6 us (9%)
  between operations  14.8 us (2%)
  other arithmetic  14.6 us (2%)
  local copies, waits for them, and re-layouts  14.1 us (2%)
    reduce_scatter x2, waiting for transfers between devices, shards(): lax.psum_scatter(jnp.einsum('jt,jbc->tbc', table_wide, adjoint, precision...  222 us
    all_gather x2, waiting for transfers between devices, shards(): lax.all_gather(field_low, 'sensors', axis=0, tiled=True)  137 us
    psum x2, blocking collectives, shards(): observed = lax.psum(observe(forward_map, spectrum, sensor_marks), 'cells')  67.6 us
    ppermute x12, starting transfers between devices, padded_2(): before = lax.ppermute(last, axis, up)  60.3 us
    dot_general x8, matrix products, spread_back(): jnp.einsum('fsc,fbs->fbc', weights, values, preferred_element_type=jnp.fl...  47.9 us
    dot_general x4, matrix products, place_cells(): jnp.einsum('fbs,cs->fbc', values, sensor_marks, preferred_element_type=jn...  44.5 us
    dot_general x8, matrix products, project(): jnp.einsum('fsc,fbc->fbs', weights, values, preferred_element_type=jnp.fl...  37 us
    dot_general x2, matrix products, shards(): jnp.einsum('jt,jbc->tbc', table_wide, adjoint, precision=lax.Precision.HI...  23.4 us
  transfers between devices with their start and end apart: 28, of which 24 were waited for; matrix products, arithmetic and copies ran while one was open for 1% of the time, Pallas kernels for 0%

commit v1 on v0

v1 whole, which is shorter than its diff:
```python
import functools
import math

import jax
import jax.numpy as jnp
import numpy as np
from jax import lax
from jax.experimental import pallas as pl
from jax.experimental.pallas import tpu as pltpu
from jax.sharding import PartitionSpec as P

MESH = pl.DeviceIdType.MESH
BF16 = jnp.bfloat16
F32 = jnp.float32
DAMPING = 0.8
ROWS = 16
HALO = 4
EXT = ROWS + 2 * HALO
STEPS = 16
COLS = 128
CELLS = ROWS * COLS
NT = 256
FB = 16
GROUPS = 8
SENS = 8
CHUNK = 2
CHUNKS = 3
JOBS = 2 * CHUNKS


def transform_tables():
    wave = np.arange(128)[:, None]
    moment = np.arange(NT)[None, :]
    phase = (wave * moment % NT).astype(np.float32) * np.float32(2.0 * math.pi / NT)
    factor = np.float32(1.0 / math.sqrt(NT))
    real = (np.cos(phase) * factor).reshape(GROUPS, 1, FB, NT)
    imag = (-np.sin(phase) * factor).reshape(GROUPS, 1, FB, NT)
    return np.concatenate([real, imag], axis=1).reshape(NT, NT)


def kernel(
    rhs_hbm,
    map_hbm,
    stiff_ref,
    react_ref,
    weight_sm,
    cell_sm,
    table_ref,
    table_t_ref,
    sol_ref,
    res_ref,
    gv,
    xg,
    spec,
    adj,
    y,
    rsib,
    rh,
    rx,
    rz,
    ms,
    oall,
    rhs_ext,
    res_ext,
    xf,
    sx,
    qx,
    c_sw,
    c_k,
    c_s,
    c_si,
    c_d,
    ua,
    ub,
    marks,
    nwt,
    loc_sem,
    init_send,
    init_recv,
    ag_send,
    ag_recv,
    sib_send,
    sib_recv,
    rh_send,
    rh_recv,
    rx_send,
    rx_recv,
    rz_send,
    rz_recv,
    o_send,
    o_recv,
    halo_send,
    halo_recv,
):
    c_me = lax.axis_index("cells")
    s_me = lax.axis_index("sensors")
    core = lax.rem(s_me, 2)
    chip = s_me // 2
    xpos = lax.rem(chip, 4)
    zpos = chip // 4

    def sidx(dz, dx, cc):
        return (lax.rem(zpos + dz, 2) * 4 + lax.rem(xpos + dx, 4)) * 2 + cc

    other = 1 - core
    sib = {"sensors": sidx(0, 0, other)}
    xp = {"sensors": sidx(0, 1, core)}
    xm = {"sensors": sidx(0, 3, core)}
    zp = {"sensors": sidx(1, 0, core)}
    cnext = {"cells": lax.rem(c_me + 1, 8)}
    cprev = {"cells": lax.rem(c_me + 7, 8)}

    def rdma(src, dst, ss, rs, dev):
        return pltpu.make_async_remote_copy(
            src_ref=src, dst_ref=dst, send_sem=ss, recv_sem=rs, device_id=dev, device_id_type=MESH
        )

    map_copies = [
        pltpu.make_async_copy(map_hbm.at[p, g], gv.at[p, g], loc_sem.at[p * GROUPS + g])
        for p in range(2)
        for g in range(GROUPS)
    ]
    rhs_copies = [
        pltpu.make_async_copy(
            rhs_hbm.at[b], rhs_ext.at[b, pl.ds(HALO, ROWS)], loc_sem.at[16 + b]
        )
        for b in range(6)
    ]
    for cp in rhs_copies:
        cp.start()
    for cp in map_copies:
        cp.start()

    barrier = pltpu.get_barrier_semaphore()
    peers = [sib, xp, xm, zp] + [{"cells": lax.rem(c_me + j, 8)} for j in range(1, 8)]
    for peer in peers:
        pl.semaphore_signal(barrier, inc=1, device_id=peer, device_id_type=MESH)
    pl.semaphore_wait(barrier, len(peers))

    def coef_copies():
        return [
            rdma(stiff_ref.at[pl.ds(8, 8)], sx.at[pl.ds(0, 8)], init_send.at[0], init_recv.at[0], cnext),
            rdma(stiff_ref.at[pl.ds(0, 8)], sx.at[pl.ds(24, 8)], init_send.at[1], init_recv.at[1], cprev),
            rdma(react_ref.at[pl.ds(8, 8)], qx.at[pl.ds(0, 8)], init_send.at[2], init_recv.at[2], cnext),
            rdma(react_ref.at[pl.ds(0, 8)], qx.at[pl.ds(24, 8)], init_send.at[3], init_recv.at[3], cprev),
        ]

    def halo_copies(ref, k, ssem, rsem):
        bs = pl.ds(k * CHUNK, CHUNK)
        return [
            rdma(
                ref.at[bs, pl.ds(ROWS, HALO)], ref.at[bs, pl.ds(0, HALO)], ssem.at[k, 0], rsem.at[k, 0], cnext
            ),
            rdma(
                ref.at[bs, pl.ds(HALO, HALO)],
                ref.at[bs, pl.ds(HALO + ROWS, HALO)],
                ssem.at[k, 1],
                rsem.at[k, 1],
                cprev,
            ),
        ]

    first = coef_copies()
    for cp in first:
        cp.start()
    for b in range(6):
        rhs_copies[b].wait()
        if b % 2 == 1:
            for cp in halo_copies(rhs_ext, b // 2, halo_send.at[0], halo_recv.at[0]):
                cp.start()

    lane = lax.broadcasted_iota(jnp.int32, (8, COLS), 1)
    acc = jnp.zeros((8, COLS), F32)
    for s in range(SENS):
        acc = jnp.where(lax.rem(lane, 8) == s, weight_sm[s_me * SENS + s], acc)
    nwt[...] = acc
    row = lax.broadcasted_iota(jnp.int32, (16, 512), 0)
    target = jnp.zeros((16, 512), jnp.int32)
    for s in range(SENS):
        target = jnp.where(lax.rem(row, 8) == s, cell_sm[s_me * SENS + s], target)
    for part in range(4):
        cell_id = lax.broadcasted_iota(jnp.int32, (16, 512), 1) + (c_me * CELLS + part * 512)
        marks[:, part * 512 : (part + 1) * 512] = jnp.where(cell_id == target, 1.0, 0.0).astype(BF16)

    sx[8:24, :] = stiff_ref[...]
    qx[8:24, :] = react_ref[...]
    for cp in first:
        cp.wait()
    erow = lax.broadcasted_iota(jnp.int32, (32, COLS), 0) + (c_me * ROWS - 8)
    inside = jnp.logical_and(erow >= 0, erow < 128)
    st = jnp.where(inside, sx[...], 0.0)
    re = jnp.where(inside, qx[...], 1.0)
    dg = re + 4.0 * st * st
    wv = DAMPING / dg
    si = jnp.where(inside, 1.0 / jnp.where(inside, st, 1.0), 0.0)
    for ref, val in ((c_sw, st * wv), (c_k, st * st * wv), (c_s, st), (c_si, si), (c_d, dg)):
        ref[...] = jnp.broadcast_to(val[8 - HALO : 8 - HALO + EXT][:, None, :], (EXT, STEPS, COLS))

    lane_s = lax.broadcasted_iota(jnp.int32, (STEPS, COLS), 1)
    not_first = lane_s > 0
    not_last = lane_s < COLS - 1

    def side_sum(v):
        n = v.shape[0]
        flat = v.reshape(n * STEPS, COLS)
        left = pltpu.roll(flat, 1, 1).reshape(v.shape)
        right = pltpu.roll(flat, COLS - 1, 1).reshape(v.shape)
        return jnp.where(not_first[None], left, 0.0) + jnp.where(not_last[None], right, 0.0)

    def precondition(src, b):
        def put(i, carry):
            rs = pl.ds(i * 4, 4)
            ua[rs] = c_sw[rs] * src[b, rs]
            return carry

        lax.fori_loop(0, EXT // 4, put, 0)
        bufs = [ua, ub, ua]
        for sweep in range(3):
            lo, hi = 1 + sweep, EXT - 1 - sweep
            now = bufs[sweep]

            def stencil(i, carry, now=now, lo=lo, sweep=sweep):
                r0 = lo + i * 2
                rs = pl.ds(r0, 2)
                mid = now[rs]
                nb = now[pl.ds(r0 + 1, 2)] + now[pl.ds(r0 - 1, 2)] + side_sum(mid)
                new = (1.0 - DAMPING) * mid + c_sw[rs] * src[b, rs] + c_k[rs] * nb
                if sweep < 2:
                    bufs[sweep + 1][rs] = new
                else:
                    xr = pl.ds(r0 - 3, 2)
                    xf[b, xr] = xf[b, xr] + c_si[rs] * new
                return carry

            lax.fori_loop(0, (hi - lo) // 2, stencil, 0)

    d_me = s_me

    def chunk_of(dz, dx, cc):
        return sidx(dz, dx, cc)

    def ag_copy(k, idx, dz, dx, cc, half, dev):
        d = chunk_of(dz, dx, cc)
        ref = xg.at[k, d] if half is None else xg.at[k, d, half]
        return rdma(ref, ref, ag_send.at[k, idx], ag_recv.at[k, idx], dev)

    def ag_sends(k):
        return {
            "sib_o": ag_copy(k, 0, 0, 0, core, None, sib),
            "xp_o": ag_copy(k, 1, 0, 0, core, None, xp),
            "xm_o": ag_copy(k, 2, 0, 0, core, None, xm),
            "zp_o": ag_copy(k, 3, 0, 0, core, None, zp),
            "xp_h": ag_copy(k, 4, 0, 3, core, 0, xp),
            "xm_h": ag_copy(k, 5, 0, 1, core, 1, xm),
            "xp_z": ag_copy(k, 6, 1, 0, core, None, xp),
            "xm_z": ag_copy(k, 7, 1, 0, core, None, xm),
            "xp_zh": ag_copy(k, 8, 1, 3, core, 0, xp),
            "xm_zh": ag_copy(k, 9, 1, 1, core, 1, xm),
            "sib_1": ag_copy(k, 10, 0, 3, core, None, sib),
            "sib_2": ag_copy(k, 11, 0, 1, core, None, sib),
            "sib_3": ag_copy(k, 12, 1, 0, core, None, sib),
            "sib_4": ag_copy(k, 13, 0, 2, core, None, sib),
            "sib_5": ag_copy(k, 14, 1, 3, core, None, sib),
            "sib_6": ag_copy(k, 15, 1, 1, core, None, sib),
            "sib_7": ag_copy(k, 16, 1, 2, core, None, sib),
        }

    def a0(u):
        k = lax.rem(u, CHUNKS)
        s = ag_sends(k)
        for name in ("xp_o", "xm_o", "zp_o", "sib_o"):
            s[name].start()

    def a1(u):
        k = lax.rem(u, CHUNKS)
        s = ag_sends(k)
        s["zp_o"].wait_recv()
        s["xp_z"].start()
        s["xm_z"].start()
        s["xp_o"].wait_recv()
        s["xp_h"].start()
        s["xm_o"].wait_recv()
        s["xm_h"].start()
        s["sib_1"].start()
        s["sib_2"].start()
        s["sib_3"].start()

    def a2(u):
        k = lax.rem(u, CHUNKS)
        s = ag_sends(k)
        s["xp_z"].wait_recv()
        s["xp_zh"].start()
        s["xm_z"].wait_recv()
        s["xm_zh"].start()
        s["xp_h"].wait_recv()
        s["xm_h"].wait_recv()
        s["sib_4"].start()
        s["sib_5"].start()
        s["sib_6"].start()

    def a3(u):
        k = lax.rem(u, CHUNKS)
        s = ag_sends(k)
        s["xp_zh"].wait_recv()
        s["xm_zh"].wait_recv()
        s["sib_7"].start()

    def a4(u):
        k = lax.rem(u, CHUNKS)
        s = ag_sends(k)
        for name in ("sib_o", "sib_1", "sib_2", "sib_3", "sib_4", "sib_5", "sib_6", "sib_7"):
            s[name].wait_recv()
        for name in s:
            s[name].wait_send()

    frow = lax.broadcasted_iota(jnp.int32, (FB, COLS), 0)
    fold = frow == lax.broadcasted_iota(jnp.int32, (FB, COLS), 1) // SENS

    def o_copies(u, k):
        return [
            rdma(
                oall.at[u, c_me], oall.at[u, c_me], o_send.at[k, j - 1], o_recv.at[u, j - 1],
                {"cells": lax.rem(c_me + j, 8)},
            )
            for j in range(1, 8)
        ]

    def observe(u):
        k = lax.rem(u, CHUNKS)

        for bb in range(CHUNK):

            def dft(rp, carry, bb=bb):
                x0 = xg[k, :, bb, 2 * rp].reshape(NT, COLS)
                x1 = xg[k, :, bb, 2 * rp + 1].reshape(NT, COLS)
                both = jnp.concatenate([x0, x1], axis=1)
                v = jnp.dot(table_ref[...], both, preferred_element_type=F32).astype(BF16)
                cols = pl.ds(pl.multiple_of(rp * 256, 256), 256)
                spec[:, bb * 32 : bb * 32 + 32, cols] = v.reshape(GROUPS, 32, 256)
                return carry

            lax.fori_loop(0, ROWS // 2, dft, 0)

        def group(g, carry):
            vg = spec[g]
            parts = []
            for p in range(2):
                o = lax.dot_general(
                    vg, gv[p, g], (((1,), (1,)), ((), ())), preferred_element_type=F32
                ).reshape(4, FB, COLS)
                parts.append(jnp.sum(jnp.where(fold[None], o, 0.0), axis=1))
            a, b = parts
            rows = []
            for bb in range(CHUNK):
                rows.append(a[2 * bb : 2 * bb + 1] - b[2 * bb + 1 : 2 * bb + 2])
                rows.append(a[2 * bb + 1 : 2 * bb + 2] + b[2 * bb : 2 * bb + 1])
            oall[u, c_me, g] = jnp.concatenate(rows, axis=0)
            return carry

        lax.fori_loop(0, GROUPS, group, 0)
        for cp in o_copies(u, k):
            cp.start()

    def sib_copies(k):
        out = {}
        for n, dx in enumerate((2, 1, 3, 0)):
            for zr in (1, 0):
                i = n * 2 + zr
                ci = sidx(zr, dx, 0) // 2
                out[(dx, zr)] = rdma(
                    y.at[k, ci * 2 + other], rsib.at[k, ci], sib_send.at[k, i], sib_recv.at[k, i], sib
                )
        return out

    def pull(u):
        k = lax.rem(u, CHUNKS)
        for cp in o_copies(u, k):
            cp.wait_recv()

        def group(g, carry):
            tot = oall[u, 0, g]
            for c in range(1, 8):
                tot = tot + oall[u, c, g]
            w = nwt[0:4] * tot
            rows = []
            for bb in range(CHUNK):
                wr = jnp.broadcast_to(w[2 * bb : 2 * bb + 1], (FB, COLS))
                wi = jnp.broadcast_to(w[2 * bb + 1 : 2 * bb + 2], (FB, COLS))
                wr = jnp.where(fold, wr, 0.0)
                wi = jnp.where(fold, wi, 0.0)
                rows.append(jnp.concatenate([wr, wi], axis=1))
                rows.append(jnp.concatenate([wi, -wr], axis=1))
            wm = jnp.concatenate(rows, axis=0).astype(BF16)
            for part in range(4):
                cols = slice(part * 512, part * 512 + 512)
                gg = jnp.concatenate([gv[0, g, :, cols], gv[1, g, :, cols]], axis=0)
                a = jnp.dot(wm, gg, preferred_element_type=F32).astype(BF16)
                jr = pl.ds(pl.multiple_of(g * 32, 32), 32)
                for bb in range(CHUNK):
                    adj[bb, jr, cols] = a[bb * 32 : bb * 32 + 32]
            return carry

        lax.fori_loop(0, GROUPS, group, 0)
        for bb in range(CHUNK):

            def idft(rp, carry, bb=bb):
                cols = pl.ds(pl.multiple_of(rp * 256, 256), 256)
                v = jnp.dot(table_t_ref[...], adj[bb, :, cols], preferred_element_type=F32).astype(BF16)
                y[k, :, bb, 2 * rp] = v[:, :COLS].reshape(16, STEPS, COLS)
                y[k, :, bb, 2 * rp + 1] = v[:, COLS:].reshape(16, STEPS, COLS)
                return carry

            lax.fori_loop(0, ROWS // 2, idft, 0)
        for cp in sib_copies(k).values():
            cp.start()

    def add_into(terms, out, dtype):
        for bb in range(CHUNK):

            def body(i, carry, bb=bb):
                rs = pl.ds(i * 4, 4)
                tot = None
                for t in terms:
                    if t[1] is None or t[1] == bb:
                        v = t[0](bb, rs).astype(F32)
                        tot = v if tot is None else tot + v
                out(bb, rs, tot.astype(dtype))
                return carry

            lax.fori_loop(0, ROWS // 4, body, 0)

    def rh_copies(k, ci, zr):
        d = ci * 2 + core
        return (
            rdma(y.at[k, d, 0], rh.at[k, 0, zr], rh_send.at[k, zr], rh_recv.at[k, zr], xp),
            rdma(y.at[k, d, 1], rh.at[k, 1, zr], rh_send.at[k, 2 + zr], rh_recv.at[k, 2 + zr], xm),
        )

    def rx_copy(k, ci, zr, side):
        d = ci * 2 + core
        i = side * 2 + zr
        return rdma(y.at[k, d], rx.at[k, side, zr], rx_send.at[k, i], rx_recv.at[k, i], (xp, xm)[side])

    def rz_copy(k):
        d = sidx(1, 0, 0) + core
        return rdma(y.at[k, d], rz.at[k], rz_send.at[k], rz_recv.at[k], zp)

    def yset(k, d):
        def out(bb, rs, v):
            y[k, d, bb, rs] = v

        return out

    def r1(u):
        k = lax.rem(u, CHUNKS)
        sc = sib_copies(k)
        for zr in (1, 0):
            ci = sidx(zr, 2, 0) // 2
            d = ci * 2 + core
            sc[(2, zr)].wait_recv()
            add_into(
                [(lambda bb, rs, d=d: y[k, d, bb, rs], None), (lambda bb, rs, ci=ci: rsib[k, ci, bb, rs], None)],
                yset(k, d),
                BF16,
            )
            for cp in rh_copies(k, ci, zr):
                cp.start()

    def r2(u):
        k = lax.rem(u, CHUNKS)
        sc = sib_copies(k)
        for zr in (1, 0):
            for side, dx in ((0, 1), (1, 3)):
                ci = sidx(zr, dx, 0) // 2
                d = ci * 2 + core
                sc[(dx, zr)].wait_recv()
                rh_copies(k, ci, zr)[side].wait_recv()
                add_into(
                    [
                        (lambda bb, rs, d=d: y[k, d, bb, rs], None),
                        (lambda bb, rs, ci=ci: rsib[k, ci, bb, rs], None),
                        (lambda bb, rs, side=side, zr=zr: rh[k, side, zr, rs], side),
                    ],
                    yset(k, d),
                    BF16,
                )
                rx_copy(k, ci, zr, side).start()

    def r3(u):
        k = lax.rem(u, CHUNKS)
        sc = sib_copies(k)

        def mset(bb, rs, v):
            ms[bb, rs] = v

        for zr in (1, 0):
            ci = sidx(zr, 0, 0) // 2
            d = ci * 2 + core
            sc[(0, zr)].wait_recv()
            rx_copy(k, ci, zr, 0).wait_recv()
            rx_copy(k, ci, zr, 1).wait_recv()
            add_into(
                [
                    (lambda bb, rs, d=d: y[k, d, bb, rs], None),
                    (lambda bb, rs, ci=ci: rsib[k, ci, bb, rs], None),
                    (lambda bb, rs, zr=zr: rx[k, 0, zr, bb, rs], None),
                    (lambda bb, rs, zr=zr: rx[k, 1, zr, bb, rs], None),
                ],
                yset(k, d) if zr == 1 else mset,
                BF16 if zr == 1 else F32,
            )
            if zr == 1:
                rz_copy(k).start()

    def r4(u):
        k = lax.rem(u, CHUNKS)
        rz_copy(k).wait_recv()
        for bb in range(CHUNK):
            b = k * CHUNK + bb

            def body(i, carry, b=b, bb=bb):
                er = pl.ds(HALO + i * 2, 2)
                rs = pl.ds(i * 2, 2)
                mid = xf[b, pl.ds(i * 2 + 1, 2)]
                um = c_s[er] * mid
                up = c_s[pl.ds(HALO + i * 2 - 1, 2)] * xf[b, rs]
                dn = c_s[pl.ds(HALO + i * 2 + 1, 2)] * xf[b, pl.ds(i * 2 + 2, 2)]
                prior = c_d[er] * mid - c_s[er] * (up + dn + side_sum(um))
                m = ms[bb, rs] + rz[k, bb, rs].astype(F32)
                r = rhs_ext[b, er] - (prior + m)
                res_ext[b, er] = r
                res_ref[b, rs] = r
                return carry

            lax.fori_loop(0, ROWS // 2, body, 0)
        for cp in halo_copies(res_ext, k, halo_send.at[1], halo_recv.at[1]):
            cp.start()
        for cp in sib_copies(k).values():
            cp.wait_send()
        for zr in (1, 0):
            for cp in rh_copies(k, 0, zr):
                cp.wait_send()
            for side in range(2):
                rx_copy(k, 0, zr, side).wait_send()
        rz_copy(k).wait_send()
        for cp in o_copies(u, k):
            cp.wait_send()

    def own_to_gather(k):
        for bb in range(CHUNK):
            b = k * CHUNK + bb

            def body(i, carry, b=b, bb=bb):
                xg[k, d_me, bb, pl.ds(i * 4, 4)] = xf[b, pl.ds(1 + i * 4, 4)].astype(BF16)
                return carry

            lax.fori_loop(0, ROWS // 4, body, 0)

    def begin(k):
        for cp in halo_copies(rhs_ext, k, halo_send.at[0], halo_recv.at[0]):
            cp.wait()
        for bb in range(CHUNK):
            b = k * CHUNK + bb
            xf[b] = jnp.zeros((ROWS + 2, STEPS, COLS), F32)
            precondition(rhs_ext, b)

    def update(k):
        for cp in halo_copies(res_ext, k, halo_send.at[1], halo_recv.at[1]):
            cp.wait()

        def body(bb, carry):
            precondition(res_ext, k * CHUNK + bb)
            return carry

        lax.fori_loop(0, CHUNK, body, 0)

    def finish_map():
        for cp in map_copies:
            cp.wait()

        def body(i, carry):
            rs = pl.ds(pl.multiple_of(lax.rem(i, 8) * 16, 16), 16)
            g = i // 8
            gv[0, g, rs] = gv[0, g, rs] + marks[...]
            return carry

        lax.fori_loop(0, 64, body, 0)

    def when_job(u, fn):
        @pl.when(jnp.logical_and(u >= 0, u < JOBS))
        def _():
            fn(u)

    def step(t, carry):
        when_job(t - 2, r1)

        @pl.when(t < CHUNKS)
        def _():
            begin(t)

        @pl.when(t >= CHUNKS)
        def _():
            update(lax.rem(t, CHUNKS))

        @pl.when(t < JOBS)
        def _():
            own_to_gather(lax.rem(t, CHUNKS))
            a0(t)

        @pl.when(t == 0)
        def _():
            finish_map()

        when_job(t - 1, observe)
        when_job(t - 2, r2)
        when_job(t, a1)
        when_job(t - 2, r3)
        when_job(t, a2)
        when_job(t - 1, pull)
        when_job(t - 2, r4)
        when_job(t, a3)
        when_job(t, a4)
        return carry

    lax.fori_loop(0, JOBS + CHUNKS, step, 0)

    def put_out(b, carry):
        sol_ref[b] = xf[b, pl.ds(1, ROWS)]
        return carry

    lax.fori_loop(0, 6, put_out, 0)


def shards(rhs, forward_map, stiffness, reaction, noise_weight, sensor_cell):
    table = transform_tables()
    rhs_t = jnp.transpose(rhs, (1, 2, 0, 3))
    maps = forward_map.reshape(2, GROUPS, FB * SENS, CELLS)
    vm = pl.BlockSpec(memory_space=pltpu.VMEM)
    sm = pl.BlockSpec(memory_space=pltpu.SMEM)
    hb = pl.BlockSpec(memory_space=pl.ANY)
    block = (CHUNK, ROWS, STEPS, COLS)
    dma = pltpu.SemaphoreType.DMA
    out = jax.ShapeDtypeStruct((6, ROWS, STEPS, COLS), F32)
    scratch = [
        pltpu.VMEM((2, GROUPS, FB * SENS, CELLS), BF16),
        pltpu.VMEM((CHUNKS, 16) + block, BF16),
        pltpu.VMEM((GROUPS, 64, CELLS), BF16),
        pltpu.VMEM((CHUNK, NT, CELLS), BF16),
        pltpu.VMEM((CHUNKS, 16) + block, BF16),
        pltpu.VMEM((CHUNKS, 8) + block, BF16),
        pltpu.VMEM((CHUNKS, 2, 2) + block[1:], BF16),
        pltpu.VMEM((CHUNKS, 2, 2) + block, BF16),
        pltpu.VMEM((CHUNKS,) + block, BF16),
        pltpu.VMEM(block, F32),
        pltpu.VMEM((JOBS, 8, GROUPS, 4, COLS), F32),
        pltpu.VMEM((6, EXT, STEPS, COLS), F32),
        pltpu.VMEM((6, EXT, STEPS, COLS), F32),
        pltpu.VMEM((6, ROWS + 2, STEPS, COLS), F32),
        pltpu.VMEM((32, COLS), F32),
        pltpu.VMEM((32, COLS), F32),
        pltpu.VMEM((EXT, STEPS, COLS), F32),
        pltpu.VMEM((EXT, STEPS, COLS), F32),
        pltpu.VMEM((EXT, STEPS, COLS), F32),
        pltpu.VMEM((EXT, STEPS, COLS), F32),
        pltpu.VMEM((EXT, STEPS, COLS), F32),
        pltpu.VMEM((EXT, STEPS, COLS), F32),
        pltpu.VMEM((EXT, STEPS, COLS), F32),
        pltpu.VMEM((16, CELLS), BF16),
        pltpu.VMEM((8, COLS), F32),
        dma((22,)),
        dma((4,)),
        dma((4,)),
        dma((CHUNKS, 17)),
        dma((CHUNKS, 17)),
        dma((CHUNKS, 8)),
        dma((CHUNKS, 8)),
        dma((CHUNKS, 4)),
        dma((CHUNKS, 4)),
        dma((CHUNKS, 4)),
        dma((CHUNKS, 4)),
        dma((CHUNKS,)),
        dma((CHUNKS,)),
        dma((CHUNKS, 7)),
        dma((JOBS, 7)),
        dma((2, CHUNKS, 2)),
        dma((2, CHUNKS, 2)),
    ]
    sol, res = pl.pallas_call(
        kernel,
        out_shape=(out, out),
        in_specs=[hb, hb, vm, vm, sm, sm, vm, vm],
        out_specs=(vm, vm),
        scratch_shapes=scratch,
        compiler_params=pltpu.CompilerParams(
            collective_id=0, has_side_effects=True, vmem_limit_bytes=60 * 1024 * 1024
        ),
    )(
        rhs_t,
        maps,
        stiffness,
        reaction,
        noise_weight,
        sensor_cell,
        jnp.asarray(table, BF16),
        jnp.asarray(table.T, BF16),
    )
    return (jnp.transpose(sol, (2, 0, 1, 3)), jnp.transpose(res, (2, 0, 1, 3)))


def solution(mesh):
    placed = (
        P("sensors", None, "cells", None),
        P(None, None, "sensors", "cells"),
        P("cells", None),
        P("cells", None),
        P(),
        P(),
    )
    return jax.shard_map(
        shards,
        mesh=mesh,
        in_specs=placed,
        out_specs=(P("sensors", None, "cells", None), P("sensors", None, "cells", None)),
        check_vma=False,
    )
```

time: 739 us -> 272 us (0.37); the launches traced: 730 us -> 271 us
  waiting for transfers between devices: 377 us -> 0 us
  Pallas kernels: 0 us -> 264 us
  matrix products: 166 us -> 0 us
  starting transfers between devices: 76.7 us -> 0 us
  blocking collectives: 67.6 us -> 0 us
  other arithmetic: 14.6 us -> 0 us
  between operations: 14.8 us -> 0.64 us
    pallas_call x0 -> x1, Pallas kernels: none -> 264 us  [shards(): pl.pallas_call(kernel, out_shape=(out, out), in_specs=[hb, hb, vm, vm, sm...]
    reduce_scatter x2 -> x0, waiting for transfers between devices: 222 us -> none  [shards(): lax.psum_scatter(jnp.einsum('jt,jbc->tbc', table_wide, adjoint, precision...]
    dot_general x28 -> x0, matrix products: 166 us -> none  [the longest x8 47.9 us: spread_back(): jnp.einsum('fsc,fbs->fbc', weights, values, preferred_element_type=jnp.fl...]
    all_gather x2 -> x0, waiting for transfers between devices: 137 us -> none  [shards(): lax.all_gather(field_low, 'sensors', axis=0, tiled=True)]
    ppermute x24 -> x0, starting transfers between devices: 75.9 us -> none  [the longest x12 60.3 us: padded_2(): before = lax.ppermute(last, axis, up)]
    psum x2 -> x0, blocking collectives: 67.6 us -> none  [shards(): observed = lax.psum(observe(forward_map, spectrum, sensor_marks), 'cells')]
    ppermute x24 -> x0, waiting for transfers between devices: 18.1 us -> none  [the longest x12 16.9 us: padded_2(): before = lax.ppermute(last, axis, up)]
  transfers between devices with their start and end apart: 28 -> 0, of which waited for: 24 -> 0; matrix products, arithmetic and copies ran while one was open for 1% -> 0% of each run, Pallas kernels for 0% -> 0%
where the time goes in v1:
time: 272 us; the launch traced here: 271 us
  Pallas kernels  264 us (97%)
  local copies, waits for them, and re-layouts  7.01 us (3%)
    pallas_call x1, Pallas kernels, shards(): pl.pallas_call(kernel, out_shape=(out, out), in_specs=[hb, hb, vm, vm, sm...  264 us
    unnamed x3, local copies, waits for them, and re-layouts  7.01 us

profile of v1, /device:TPU:0, one launch (start us, length us, event | category | flops | bytes accessed | tf_op | source)
XLA Modules:
  0.0 271.3 jit_solution(2308141098068372823)
XLA Ops:
  0.6 2.5 copy.14
  3.1 263.6 %shard_map.95 = (f32[6,16,16,128]{3,2,1,0:T(8,128)}, f32[6,16,16,128]{3,2,1,0:T(8,128)}) custom-call(f32[6,16,16,128]{3,2,1,0:T(8,128)} %bitcast.7, bf16[2,8,128,2048]{3,2,1,0:T(8,128)(2,1)} %bitcast.6, f32[16,128]{1,0:T(8,128)} %stiff_ref.1, f32[16,128]{1,0:T(8,128)} %react_ref.1, f32[128]{0:T(128)} %weight_sm.1, s32[128]{0:T(128)} %cell_sm.1, ...), custom_call_target="tpu_custom_call" | custom-call | tf_op jit(solution)/shard_map/pallas_call | solution.py:688
  266.7 2.3 copy.11
  269.0 2.3 copy.12

commit v2 on v1

v2 whole, which is shorter than its diff:
```python
import functools
import math

import jax
import jax.numpy as jnp
import numpy as np
from jax import lax
from jax.experimental import pallas as pl
from jax.experimental.pallas import tpu as pltpu
from jax.sharding import PartitionSpec as P

MESH = pl.DeviceIdType.MESH
BF16 = jnp.bfloat16
F32 = jnp.float32
DAMPING = 0.8
ROWS = 16
HALO = 4
EXT = ROWS + 2 * HALO
STEPS = 16
COLS = 128
CELLS = ROWS * COLS
NT = 256
FB = 16
GROUPS = 8
SENS = 8
CHUNK = 1
CHUNKS = 6 // CHUNK
SPLIT = 8
FIRST = pl.ds(0, SPLIT)
REST = pl.ds(SPLIT, ROWS - SPLIT)
ORDER = (
    ("update", 0), ("a2", 2), ("a0", 0), ("a1", 1), ("pull", 3), ("r3", 5),
    ("a3", 2), ("observe", 2), ("r2", 4), ("r1", 3),
)
JOBS = 2 * CHUNKS


def transform_tables():
    wave = np.arange(128)[:, None]
    moment = np.arange(NT)[None, :]
    phase = (wave * moment % NT).astype(np.float32) * np.float32(2.0 * math.pi / NT)
    factor = np.float32(1.0 / math.sqrt(NT))
    real = (np.cos(phase) * factor).reshape(GROUPS, 1, FB, NT)
    imag = (-np.sin(phase) * factor).reshape(GROUPS, 1, FB, NT)
    return np.concatenate([real, imag], axis=1).reshape(NT, NT)


def kernel(
    rhs_hbm,
    map_hbm,
    stiff_ref,
    react_ref,
    weight_sm,
    cell_sm,
    table_ref,
    table_t_ref,
    sol_ref,
    res_ref,
    gv,
    xg,
    spec,
    adj,
    y,
    rsib,
    rzf,
    rxg,
    rxf,
    rzg,
    oall,
    rhs_ext,
    res_ext,
    xf,
    sx,
    qx,
    c_sw,
    c_k,
    c_s,
    c_si,
    c_d,
    marks,
    nwt,
    loc_sem,
    init_send,
    init_recv,
    ag_send,
    ag_recv,
    sib_send,
    sib_recv,
    rzf_send,
    rzf_recv,
    rxg_send,
    rxg_recv,
    rxf_send,
    rxf_recv,
    rzg_send,
    rzg_recv,
    o_send,
    o_recv,
    halo_send,
    halo_recv,
):
    c_me = lax.axis_index("cells")
    s_me = lax.axis_index("sensors")
    core = lax.rem(s_me, 2)
    chip = s_me // 2
    xpos = lax.rem(chip, 4)
    zpos = chip // 4

    def sidx(dz, dx, cc):
        return (lax.rem(zpos + dz, 2) * 4 + lax.rem(xpos + dx, 4)) * 2 + cc

    other = 1 - core
    sib = {"sensors": sidx(0, 0, other)}
    xp = {"sensors": sidx(0, 1, core)}
    xm = {"sensors": sidx(0, 3, core)}
    zp = {"sensors": sidx(1, 0, core)}
    xd = {"sensors": sidx(0, 2, core)}
    xto = {1: xp, 2: xd, 3: xm}
    cnext = {"cells": lax.rem(c_me + 1, 8)}
    cprev = {"cells": lax.rem(c_me + 7, 8)}

    def rdma(src, dst, ss, rs, dev):
        return pltpu.make_async_remote_copy(
            src_ref=src, dst_ref=dst, send_sem=ss, recv_sem=rs, device_id=dev, device_id_type=MESH
        )

    map_copies = [
        pltpu.make_async_copy(map_hbm.at[p, g], gv.at[p, g], loc_sem.at[p * GROUPS + g])
        for p in range(2)
        for g in range(GROUPS)
    ]
    rhs_copies = [
        pltpu.make_async_copy(
            rhs_hbm.at[b], rhs_ext.at[b, pl.ds(HALO, ROWS)], loc_sem.at[16 + b]
        )
        for b in range(6)
    ]
    for cp in rhs_copies:
        cp.start()
    for cp in map_copies:
        cp.start()

    barrier = pltpu.get_barrier_semaphore()
    peers = [sib, xp, xm, xd, zp] + [{"cells": lax.rem(c_me + j, 8)} for j in range(1, 8)]
    for peer in peers:
        pl.semaphore_signal(barrier, inc=1, device_id=peer, device_id_type=MESH)
    pl.semaphore_wait(barrier, len(peers))

    def coef_copies():
        return [
            rdma(stiff_ref.at[pl.ds(8, 8)], sx.at[pl.ds(0, 8)], init_send.at[0], init_recv.at[0], cnext),
            rdma(stiff_ref.at[pl.ds(0, 8)], sx.at[pl.ds(24, 8)], init_send.at[1], init_recv.at[1], cprev),
            rdma(react_ref.at[pl.ds(8, 8)], qx.at[pl.ds(0, 8)], init_send.at[2], init_recv.at[2], cnext),
            rdma(react_ref.at[pl.ds(0, 8)], qx.at[pl.ds(24, 8)], init_send.at[3], init_recv.at[3], cprev),
        ]

    def halo_copies(ref, k, ssem, rsem):
        bs = pl.ds(k * CHUNK, CHUNK)
        return [
            rdma(
                ref.at[bs, pl.ds(ROWS, HALO)], ref.at[bs, pl.ds(0, HALO)], ssem.at[k, 0], rsem.at[k, 0], cnext
            ),
            rdma(
                ref.at[bs, pl.ds(HALO, HALO)],
                ref.at[bs, pl.ds(HALO + ROWS, HALO)],
                ssem.at[k, 1],
                rsem.at[k, 1],
                cprev,
            ),
        ]

    first = coef_copies()
    for cp in first:
        cp.start()
    for b in range(6):
        rhs_copies[b].wait()
        if b % CHUNK == CHUNK - 1:
            for cp in halo_copies(rhs_ext, b // CHUNK, halo_send.at[0], halo_recv.at[0]):
                cp.start()

    lane = lax.broadcasted_iota(jnp.int32, (8, COLS), 1)
    acc = jnp.zeros((8, COLS), F32)
    for s in range(SENS):
        acc = jnp.where(lax.rem(lane, 8) == s, weight_sm[s_me * SENS + s], acc)
    nwt[...] = acc
    row = lax.broadcasted_iota(jnp.int32, (16, 512), 0)
    target = jnp.zeros((16, 512), jnp.int32)
    for s in range(SENS):
        target = jnp.where(lax.rem(row, 8) == s, cell_sm[s_me * SENS + s], target)
    for part in range(4):
        cell_id = lax.broadcasted_iota(jnp.int32, (16, 512), 1) + (c_me * CELLS + part * 512)
        marks[:, part * 512 : (part + 1) * 512] = jnp.where(cell_id == target, 1.0, 0.0).astype(BF16)

    sx[8:24, :] = stiff_ref[...]
    qx[8:24, :] = react_ref[...]
    for cp in first:
        cp.wait()
    erow = lax.broadcasted_iota(jnp.int32, (32, COLS), 0) + (c_me * ROWS - 8)
    inside = jnp.logical_and(erow >= 0, erow < 128)
    st = jnp.where(inside, sx[...], 0.0)
    re = jnp.where(inside, qx[...], 1.0)
    dg = re + 4.0 * st * st
    wv = DAMPING / dg
    si = jnp.where(inside, 1.0 / jnp.where(inside, st, 1.0), 0.0)
    for ref, val in ((c_sw, st * wv), (c_k, st * st * wv), (c_s, st), (c_si, si), (c_d, dg)):
        ref[...] = jnp.broadcast_to(val[8 - HALO : 8 - HALO + EXT][:, None, :], (EXT, STEPS, COLS))

    lane_s = lax.broadcasted_iota(jnp.int32, (STEPS, COLS), 1)
    not_first = lane_s > 0
    not_last = lane_s < COLS - 1

    def sides(v):
        left = pltpu.roll(v, 1, 1)
        right = pltpu.roll(v, COLS - 1, 1)
        return jnp.where(not_first, left, 0.0) + jnp.where(not_last, right, 0.0)

    def precondition(src, b, mode):
        levels = [{}, {}, {}]
        first = {}
        for r in range(EXT + 3):
            if r < EXT:
                first[r] = c_sw[r] * src[b, r]
                levels[0][r] = first[r]
            for n in range(3):
                q = r - 1 - n
                if not n + 1 <= q <= EXT - 2 - n:
                    continue
                now = levels[n]
                nb = now[q - 1] + now[q + 1] + sides(now[q])
                new = (1.0 - DAMPING) * now[q] + first[q] + c_k[q] * nb
                if n < 2:
                    levels[n + 1][q] = new
                elif mode == 0:
                    xf[b, q - 3] = c_si[q] * new
                elif mode == 1:
                    xf[b, q - 3] = xf[b, q - 3] + c_si[q] * new
                elif HALO <= q < HALO + ROWS:
                    sol_ref[b, q - HALO] = xf[b, q - 3] + c_si[q] * new

    d_me = s_me

    def ag_copy(k, idx, dz, dx, rows, dev):
        d = sidx(dz, dx, core)
        ref = xg.at[k, d] if rows is None else xg.at[k, d, :, rows]
        return rdma(ref, ref, ag_send.at[k, idx], ag_recv.at[k, idx], dev)

    def ag_copies(k):
        table = [
            (0, 0, None, sib),
            (0, 0, None, xp),
            (0, 0, None, xm),
            (0, 0, None, xd),
            (0, 0, None, zp),
            (1, 0, REST, xp),
            (1, 0, REST, xm),
            (1, 0, REST, xd),
            (0, 3, FIRST, zp),
            (0, 1, FIRST, zp),
            (0, 2, FIRST, zp),
            (0, 3, None, sib),
            (0, 1, None, sib),
            (0, 2, None, sib),
            (1, 0, None, sib),
            (1, 3, None, sib),
            (1, 1, None, sib),
            (1, 2, None, sib),
        ]
        return [ag_copy(k, i, *row) for i, row in enumerate(table)]

    def a0(u):
        k = lax.rem(u, CHUNKS)
        own_to_gather(k)
        s = ag_copies(k)
        for i in (4, 1, 2, 3, 0):
            s[i].start()

    def a1(u):
        s = ag_copies(lax.rem(u, CHUNKS))
        s[4].wait_recv()
        for i in (5, 6, 7, 14):
            s[i].start()
        for i, z, f in ((1, 8, 11), (2, 9, 12), (3, 10, 13)):
            s[i].wait_recv()
            s[z].start()
            s[f].start()

    def a2(u):
        s = ag_copies(lax.rem(u, CHUNKS))
        for i, z, f in ((5, 8, 15), (6, 9, 16), (7, 10, 17)):
            s[i].wait_recv()
            s[z].wait_recv()
            s[f].start()

    def a3(u):
        s = ag_copies(lax.rem(u, CHUNKS))
        for i in (0, 11, 12, 13, 14, 15, 16, 17):
            s[i].wait_recv()
        for cp in s:
            cp.wait_send()

    frow = lax.broadcasted_iota(jnp.int32, (FB, COLS), 0)
    fold = frow == lax.broadcasted_iota(jnp.int32, (FB, COLS), 1) // SENS

    def o_copies(u, k):
        return [
            rdma(
                oall.at[u, c_me], oall.at[u, c_me], o_send.at[k, j - 1], o_recv.at[u, j - 1],
                {"cells": lax.rem(c_me + j, 8)},
            )
            for j in range(1, 8)
        ]

    def observe(u):
        k = lax.rem(u, CHUNKS)

        for bb in range(CHUNK):

            def dft(rp, carry, bb=bb):
                x0 = xg[k, :, bb, 2 * rp].reshape(NT, COLS)
                x1 = xg[k, :, bb, 2 * rp + 1].reshape(NT, COLS)
                both = jnp.concatenate([x0, x1], axis=1)
                v = jnp.dot(table_ref[...], both, preferred_element_type=F32).astype(BF16)
                cols = pl.ds(pl.multiple_of(rp * 256, 256), 256)
                spec[:, bb * 32 : bb * 32 + 32, cols] = v.reshape(GROUPS, 32, 256)
                return carry

            lax.fori_loop(0, ROWS // 2, dft, 0, unroll=8)

        def group(g, carry):
            vg = spec[g]
            parts = []
            for p in range(2):
                o = lax.dot_general(
                    vg, gv[p, g], (((1,), (1,)), ((), ())), preferred_element_type=F32
                ).reshape(2 * CHUNK, FB, COLS)
                parts.append(jnp.sum(jnp.where(fold[None], o, 0.0), axis=1))
            a, b = parts
            rows = []
            for bb in range(CHUNK):
                rows.append(a[2 * bb : 2 * bb + 1] - b[2 * bb + 1 : 2 * bb + 2])
                rows.append(a[2 * bb + 1 : 2 * bb + 2] + b[2 * bb : 2 * bb + 1])
            oall[u, c_me, g] = jnp.concatenate(rows, axis=0)
            return carry

        lax.fori_loop(0, GROUPS, group, 0, unroll=4)
        for cp in o_copies(u, k):
            cp.start()

    def sib_copy(k):
        return rdma(y.at[k, other], rsib.at[k], sib_send.at[k], sib_recv.at[k], sib)

    def pull(u):
        k = lax.rem(u, CHUNKS)
        for cp in o_copies(u, k):
            cp.wait_recv()

        def group(g, carry):
            tot = oall[u, 0, g]
            for c in range(1, 8):
                tot = tot + oall[u, c, g]
            w = nwt[0 : 2 * CHUNK] * tot
            rows = []
            for bb in range(CHUNK):
                wr = jnp.broadcast_to(w[2 * bb : 2 * bb + 1], (FB, COLS))
                wi = jnp.broadcast_to(w[2 * bb + 1 : 2 * bb + 2], (FB, COLS))
                wr = jnp.where(fold, wr, 0.0)
                wi = jnp.where(fold, wi, 0.0)
                rows.append(jnp.concatenate([wr, wi], axis=1))
                rows.append(jnp.concatenate([wi, -wr], axis=1))
            wm = jnp.concatenate(rows, axis=0).astype(BF16)
            for part in range(4):
                cols = slice(part * 512, part * 512 + 512)
                gg = jnp.concatenate([gv[0, g, :, cols], gv[1, g, :, cols]], axis=0)
                a = jnp.dot(wm, gg, preferred_element_type=F32).astype(BF16)
                jr = pl.ds(pl.multiple_of(g * 32, 32), 32)
                for bb in range(CHUNK):
                    adj[bb, jr, cols] = a[bb * 32 : bb * 32 + 32]
            return carry

        lax.fori_loop(0, GROUPS, group, 0, unroll=4)
        for bb in range(CHUNK):

            def idft(rp, carry, bb=bb):
                cols = pl.ds(pl.multiple_of(rp * 256, 256), 256)
                v = jnp.dot(table_t_ref[...], adj[bb, :, cols], preferred_element_type=F32).astype(BF16)
                for half in range(2):
                    w = v[:, half * COLS : half * COLS + COLS].reshape(8, 2, STEPS, COLS)
                    for c in range(2):
                        y[k, c, :, bb, 2 * rp + half] = w[:, c]
                return carry

            lax.fori_loop(0, ROWS // 2, idft, 0, unroll=8)
        sib_copy(k).start()

    def block(zr, dx):
        return sidx(zr, dx, 0) // 2

    def total(k, zr, dx, bb, rs, arrived):
        ci = block(zr, dx)
        tot = y[k, core, ci, bb, rs].astype(F32) + rsib[k, ci, bb, rs].astype(F32)
        for ref in arrived:
            tot = tot + ref[bb, rs].astype(F32)
        return tot

    def add_rows(k, zr, dx, lo, hi, arrived):
        for bb in range(CHUNK):
            for r in range(lo, hi, 2):
                rs = pl.ds(r, 2)
                y[k, core, block(zr, dx), bb, rs] = total(k, zr, dx, bb, rs, arrived).astype(BF16)

    def rzf_copy(k, dx):
        return rdma(
            y.at[k, core, block(1, dx), :, FIRST], rzf.at[k, dx, :, FIRST], rzf_send.at[k, dx], rzf_recv.at[k, dx], zp
        )

    def rxg_copy(k, zr, dx):
        i = zr * 3 + dx - 1
        return rdma(
            y.at[k, core, block(zr, dx), :, REST], rxg.at[k, i, :, REST], rxg_send.at[k, i], rxg_recv.at[k, i], xto[dx]
        )

    def rxf_copy(k, dx):
        i = dx - 1
        return rdma(
            y.at[k, core, block(0, dx), :, FIRST], rxf.at[k, i, :, FIRST], rxf_send.at[k, i], rxf_recv.at[k, i], xto[dx]
        )

    def rzg_copy(k):
        return rdma(
            y.at[k, core, block(1, 0), :, REST], rzg.at[k, :, REST], rzg_send.at[k], rzg_recv.at[k], zp
        )

    def r1(u):
        k = lax.rem(u, CHUNKS)
        sib_copy(k).wait_recv()
        for dx in (2, 1, 3):
            add_rows(k, 1, dx, 0, SPLIT, ())
            rzf_copy(k, dx).start()
            add_rows(k, 1, dx, SPLIT, ROWS, ())
            rxg_copy(k, 1, dx).start()
        add_rows(k, 1, 0, 0, SPLIT, ())
        rzf_copy(k, 0).start()
        for dx in (2, 1, 3):
            add_rows(k, 0, dx, SPLIT, ROWS, ())
            rxg_copy(k, 0, dx).start()

    def r2(u):
        k = lax.rem(u, CHUNKS)
        for dx in (2, 1, 3):
            rzf_copy(k, dx).wait_recv()
            add_rows(k, 0, dx, 0, SPLIT, (rzf.at[k, dx],))
            rxf_copy(k, dx).start()
        for dx in (1, 3, 2):
            rxg_copy(k, 1, dx).wait_recv()
        add_rows(k, 1, 0, SPLIT, ROWS, [rxg.at[k, 3 + i] for i in range(3)])
        rzg_copy(k).start()

    def r3(u):
        k = lax.rem(u, CHUNKS)
        rzf_copy(k, 0).wait_recv()
        for dx in (1, 3, 2):
            rxg_copy(k, 0, dx).wait_recv()
            rxf_copy(k, dx).wait_recv()
        rzg_copy(k).wait_recv()
        for bb in range(CHUNK):
            b = k * CHUNK + bb
            for i in range(0, ROWS, 2):
                er = pl.ds(HALO + i, 2)
                rs = pl.ds(i, 2)
                us = [c_s[HALO + i - 1 + n] * xf[b, i + n] for n in range(4)]
                if i < SPLIT:
                    arrived = [rzf.at[k, 0]] + [rxf.at[k, n] for n in range(3)]
                else:
                    arrived = [rzg.at[k]] + [rxg.at[k, n] for n in range(3)]
                m = total(k, 0, 0, bb, rs, arrived)
                for n in range(2):
                    e = HALO + i + n
                    nb = us[n] + us[n + 2] + sides(us[n + 1])
                    prior = c_d[e] * xf[b, i + n + 1] - c_s[e] * nb
                    r = rhs_ext[b, e] - (prior + m[n])
                    res_ext[b, e] = r
                    res_ref[b, i + n] = r
        for cp in halo_copies(res_ext, k, halo_send.at[1], halo_recv.at[1]):
            cp.start()
        sib_copy(k).wait_send()
        for dx in range(4):
            rzf_copy(k, dx).wait_send()
        for dx in (1, 2, 3):
            rxf_copy(k, dx).wait_send()
            for zr in range(2):
                rxg_copy(k, zr, dx).wait_send()
        rzg_copy(k).wait_send()
        for cp in o_copies(u, k):
            cp.wait_send()

    def own_to_gather(k):
        for bb in range(CHUNK):
            b = k * CHUNK + bb

            def body(i, carry, b=b, bb=bb):
                xg[k, d_me, bb, pl.ds(i * 4, 4)] = xf[b, pl.ds(1 + i * 4, 4)].astype(BF16)
                return carry

            lax.fori_loop(0, ROWS // 4, body, 0, unroll=4)

    def begin(k):
        for cp in halo_copies(rhs_ext, k, halo_send.at[0], halo_recv.at[0]):
            cp.wait()
        for bb in range(CHUNK):
            b = k * CHUNK + bb
            precondition(rhs_ext, b, 0)

    def update(k, mode):
        for cp in halo_copies(res_ext, k, halo_send.at[1], halo_recv.at[1]):
            cp.wait()

        for bb in range(CHUNK):
            precondition(res_ext, k * CHUNK + bb, mode)

    def finish_map():
        for cp in map_copies:
            cp.wait()

        def body(i, carry):
            rs = pl.ds(pl.multiple_of(lax.rem(i, 8) * 16, 16), 16)
            g = i // 8
            gv[0, g, rs] = gv[0, g, rs] + marks[...]
            return carry

        lax.fori_loop(0, 64, body, 0, unroll=4)

    def advance(u):
        @pl.when(u < CHUNKS)
        def _():
            begin(u)

        @pl.when(jnp.logical_and(u >= CHUNKS, u < JOBS))
        def _():
            update(lax.rem(u, CHUNKS), 1)

        @pl.when(u >= JOBS)
        def _():
            update(lax.rem(u, CHUNKS), 2)

    stages = {
        "a0": a0, "a1": a1, "a2": a2, "a3": a3, "observe": observe, "pull": pull, "r1": r1, "r2": r2, "r3": r3
    }

    def step(t, carry):
        for name, late in ORDER:
            u = t - late
            if name == "update":
                advance(u)
                continue

            @pl.when(jnp.logical_and(u >= 0, u < JOBS))
            def _(name=name, u=u):
                stages[name](u)

            if name == "a0":

                @pl.when(t == 1)
                def _():
                    finish_map()

        return carry

    lax.fori_loop(0, JOBS + CHUNKS, step, 0)


def shards(rhs, forward_map, stiffness, reaction, noise_weight, sensor_cell):
    table = transform_tables()
    rhs_t = jnp.transpose(rhs, (1, 2, 0, 3))
    maps = forward_map.reshape(2, GROUPS, FB * SENS, CELLS)
    vm = pl.BlockSpec(memory_space=pltpu.VMEM)
    sm = pl.BlockSpec(memory_space=pltpu.SMEM)
    hb = pl.BlockSpec(memory_space=pl.ANY)
    block = (CHUNK, ROWS, STEPS, COLS)
    dma = pltpu.SemaphoreType.DMA
    out = jax.ShapeDtypeStruct((6, ROWS, STEPS, COLS), F32)
    scratch = [
        pltpu.VMEM((2, GROUPS, FB * SENS, CELLS), BF16),
        pltpu.VMEM((CHUNKS, 16) + block, BF16),
        pltpu.VMEM((GROUPS, 32 * CHUNK, CELLS), BF16),
        pltpu.VMEM((CHUNK, NT, CELLS), BF16),
        pltpu.VMEM((CHUNKS, 2, 8) + block, BF16),
        pltpu.VMEM((CHUNKS, 8) + block, BF16),
        pltpu.VMEM((CHUNKS, 4) + block, BF16),
        pltpu.VMEM((CHUNKS, 6) + block, BF16),
        pltpu.VMEM((CHUNKS, 3) + block, BF16),
        pltpu.VMEM((CHUNKS,) + block, BF16),
        pltpu.VMEM((JOBS, 8, GROUPS, 2 * CHUNK, COLS), F32),
        pltpu.VMEM((6, EXT, STEPS, COLS), F32),
        pltpu.VMEM((6, EXT, STEPS, COLS), F32),
        pltpu.VMEM((6, ROWS + 2, STEPS, COLS), F32),
        pltpu.VMEM((32, COLS), F32),
        pltpu.VMEM((32, COLS), F32),
        pltpu.VMEM((EXT, STEPS, COLS), F32),
        pltpu.VMEM((EXT, STEPS, COLS), F32),
        pltpu.VMEM((EXT, STEPS, COLS), F32),
        pltpu.VMEM((EXT, STEPS, COLS), F32),
        pltpu.VMEM((EXT, STEPS, COLS), F32),
        pltpu.VMEM((16, CELLS), BF16),
        pltpu.VMEM((8, COLS), F32),
        dma((22,)),
        dma((4,)),
        dma((4,)),
        dma((CHUNKS, 18)),
        dma((CHUNKS, 18)),
        dma((CHUNKS,)),
        dma((CHUNKS,)),
        dma((CHUNKS, 4)),
        dma((CHUNKS, 4)),
        dma((CHUNKS, 6)),
        dma((CHUNKS, 6)),
        dma((CHUNKS, 3)),
        dma((CHUNKS, 3)),
        dma((CHUNKS,)),
        dma((CHUNKS,)),
        dma((CHUNKS, 7)),
        dma((JOBS, 7)),
        dma((2, CHUNKS, 2)),
        dma((2, CHUNKS, 2)),
    ]
    sol, res = pl.pallas_call(
        kernel,
        out_shape=(out, out),
        in_specs=[hb, hb, vm, vm, sm, sm, vm, vm],
        out_specs=(vm, vm),
        scratch_shapes=scratch,
        compiler_params=pltpu.CompilerParams(
            collective_id=0, has_side_effects=True, vmem_limit_bytes=60 * 1024 * 1024
        ),
    )(
        rhs_t,
        maps,
        stiffness,
        reaction,
        noise_weight,
        sensor_cell,
        jnp.asarray(table, BF16),
        jnp.asarray(table.T, BF16),
    )
    return (jnp.transpose(sol, (2, 0, 1, 3)), jnp.transpose(res, (2, 0, 1, 3)))


def solution(mesh):
    placed = (
        P("sensors", None, "cells", None),
        P(None, None, "sensors", "cells"),
        P("cells", None),
        P("cells", None),
        P(),
        P(),
    )
    return jax.shard_map(
        shards,
        mesh=mesh,
        in_specs=placed,
        out_specs=(P("sensors", None, "cells", None), P("sensors", None, "cells", None)),
        check_vma=False,
    )
```

time: 272 us -> 174 us (0.64)
  Pallas kernels: 264 us -> 166 us
    pallas_call x1, Pallas kernels: 264 us -> 166 us  [shards(): pl.pallas_call(kernel, out_shape=(out, out), in_specs=[hb, hb, vm, vm, sm...]
where the time goes in v2:
time: 174 us
  Pallas kernels  166 us (95%)
  local copies, waits for them, and re-layouts  7.01 us (4%)
    pallas_call x1, Pallas kernels, shards(): pl.pallas_call(kernel, out_shape=(out, out), in_specs=[hb, hb, vm, vm, sm...  166 us
    unnamed x3, local copies, waits for them, and re-layouts  7.01 us

profile of v2, /device:TPU:0, one launch (start us, length us, event | category | flops | bytes accessed | tf_op | source)
XLA Modules:
  0.0 174.0 jit_solution(5009975683018338826)
XLA Ops:
  0.6 2.5 %copy.14 = f32[16,6,16,128]{3,0,2,1:T(8,128)} copy(f32[16,6,16,128]{3,2,1,0:T(8,128)} %param.8) | data formatting | bytes 1572864 | tf_op args[0]
  3.1 166.4 %shard_map.95 = (f32[6,16,16,128]{3,2,1,0:T(8,128)}, f32[6,16,16,128]{3,2,1,0:T(8,128)}) custom-call(f32[6,16,16,128]{3,2,1,0:T(8,128)} %bitcast.7, bf16[2,8,128,2048]{3,2,1,0:T(8,128)(2,1)} %bitcast.6, f32[16,128]{1,0:T(8,128)} %stiff_ref.1, f32[16,128]{1,0:T(8,128)} %react_ref.1, f32[128]{0:T(128)} %weight_sm.1, s32[128]{0:T(128)} %cell_sm.1, ...), custom_call_target="tpu_custom_call" | custom-call | tf_op jit(solution)/shard_map/pallas_call | solution.py:625
  169.5 2.3 %copy.11 = f32[16,6,16,128]{3,2,1,0:T(8,128)} copy(f32[16,6,16,128]{3,0,2,1:T(8,128)} %bitcast.9) | data formatting | bytes 1572864
  171.8 2.3 %copy.12 = f32[16,6,16,128]{3,2,1,0:T(8,128)} copy(f32[16,6,16,128]{3,0,2,1:T(8,128)} %bitcast.8) | data formatting | bytes 1572864

commit v3 on v2

--- a/solution.py
+++ b/solution.py
@@ -28,9 +28,33 @@
 SPLIT = 8
 FIRST = pl.ds(0, SPLIT)
 REST = pl.ds(SPLIT, ROWS - SPLIT)
+PASS = 2
+PASSES = 12 // PASS
 ORDER = (
-    ("update", 0), ("a2", 2), ("a0", 0), ("a1", 1), ("pull", 3), ("r3", 5),
-    ("a3", 2), ("observe", 2), ("r2", 4), ("r1", 3),
+    ("update", 0, 0),
+    ("a0", 0, 0),
+    ("a2", 0, 1),
+    ("idft", 1, 2),
+    ("r1", 0, 2),
+    ("a2", 1, 1),
+    ("a3", 0, 1),
+    ("dft", 0, 1),
+    ("r1", 1, 2),
+    ("a3", 1, 1),
+    ("dft", 1, 1),
+    ("oa", 0, 1),
+    ("ob", 0, 1),
+    ("r2", 0, 2),
+    ("update", 1, 0),
+    ("a0", 1, 0),
+    ("r2", 1, 2),
+    ("a1", 0, 0),
+    ("r3", 0, 2),
+    ("pa", 0, 1),
+    ("pb", 0, 1),
+    ("a1", 1, 0),
+    ("idft", 0, 1),
+    ("r3", 1, 2),
 )
 JOBS = 2 * CHUNKS
 
@@ -69,9 +93,13 @@
     oall,
     rhs_ext,
     res_ext,
+    hin,
+    hout,
+    stage,
     xf,
     sx,
     qx,
+    sxin,
     c_sw,
     c_k,
     c_s,
@@ -80,20 +108,11 @@
     marks,
     nwt,
     loc_sem,
-    init_send,
-    init_recv,
+    init_sem,
     ag_send,
     ag_recv,
-    sib_send,
-    sib_recv,
-    rzf_send,
-    rzf_recv,
-    rxg_send,
-    rxg_recv,
-    rxf_send,
-    rxf_recv,
-    rzg_send,
-    rzg_recv,
+    rs_send,
+    rs_recv,
     o_send,
     o_recv,
     halo_send,
@@ -124,14 +143,17 @@
             src_ref=src, dst_ref=dst, send_sem=ss, recv_sem=rs, device_id=dev, device_id_type=MESH
         )
 
+    def drain(ref, sem):
+        pltpu.make_async_copy(ref, ref, sem).wait()
+
     map_copies = [
-        pltpu.make_async_copy(map_hbm.at[p, g], gv.at[p, g], loc_sem.at[p * GROUPS + g])
+        pltpu.make_async_copy(map_hbm.at[p, g], gv.at[p, g], loc_sem.at[6])
         for p in range(2)
         for g in range(GROUPS)
     ]
     rhs_copies = [
         pltpu.make_async_copy(
-            rhs_hbm.at[b], rhs_ext.at[b, pl.ds(HALO, ROWS)], loc_sem.at[16 + b]
+            rhs_hbm.at[:, b], stage.at[b], loc_sem.at[b]
         )
         for b in range(6)
     ]
@@ -148,35 +170,32 @@
 
     def coef_copies():
         return [
-            rdma(stiff_ref.at[pl.ds(8, 8)], sx.at[pl.ds(0, 8)], init_send.at[0], init_recv.at[0], cnext),
-            rdma(stiff_ref.at[pl.ds(0, 8)], sx.at[pl.ds(24, 8)], init_send.at[1], init_recv.at[1], cprev),
-            rdma(react_ref.at[pl.ds(8, 8)], qx.at[pl.ds(0, 8)], init_send.at[2], init_recv.at[2], cnext),
-            rdma(react_ref.at[pl.ds(0, 8)], qx.at[pl.ds(24, 8)], init_send.at[3], init_recv.at[3], cprev),
+            rdma(stiff_ref.at[pl.ds(8, 8)], sxin.at[0], init_sem.at[0], init_sem.at[1], cnext),
+            rdma(stiff_ref.at[pl.ds(0, 8)], sxin.at[1], init_sem.at[0], init_sem.at[1], cprev),
+            rdma(react_ref.at[pl.ds(8, 8)], sxin.at[2], init_sem.at[0], init_sem.at[1], cnext),
+            rdma(react_ref.at[pl.ds(0, 8)], sxin.at[3], init_sem.at[0], init_sem.at[1], cprev),
         ]
 
-    def halo_copies(ref, k, ssem, rsem):
-        bs = pl.ds(k * CHUNK, CHUNK)
-        return [
-            rdma(
-                ref.at[bs, pl.ds(ROWS, HALO)], ref.at[bs, pl.ds(0, HALO)], ssem.at[k, 0], rsem.at[k, 0], cnext
-            ),
-            rdma(
-                ref.at[bs, pl.ds(HALO, HALO)],
-                ref.at[bs, pl.ds(HALO + ROWS, HALO)],
-                ssem.at[k, 1],
-                rsem.at[k, 1],
-                cprev,
-            ),
-        ]
+    def halo_start(ref, phase, k):
+        for n, lo, dev in ((0, ROWS, cnext), (1, HALO, cprev)):
+            hout[phase, k, n] = ref[k, pl.ds(lo, HALO)].astype(BF16)
+            rdma(hout.at[phase, k, n], hin.at[phase, k, n], halo_send.at[phase, k], halo_recv.at[phase, k], dev).start()
+
+    def halo_finish(ref, phase, k):
+        drain(hin.at[phase, k], halo_recv.at[phase, k])
+        drain(hout.at[phase, k], halo_send.at[phase, k])
+        for n, lo in ((0, 0), (1, HALO + ROWS)):
+            ref[k, pl.ds(lo, HALO)] = hin[phase, k, n].astype(F32)
 
     first = coef_copies()
     for cp in first:
         cp.start()
     for b in range(6):
         rhs_copies[b].wait()
-        if b % CHUNK == CHUNK - 1:
-            for cp in halo_copies(rhs_ext, b // CHUNK, halo_send.at[0], halo_recv.at[0]):
-                cp.start()
+        flat = stage.at[b].reshape(STEPS * ROWS, COLS)
+        for r in range(ROWS):
+            rhs_ext[b, HALO + r] = flat[pl.ds(r, STEPS, stride=ROWS), :]
+        halo_start(rhs_ext, 0, b)
 
     lane = lax.broadcasted_iota(jnp.int32, (8, COLS), 1)
     acc = jnp.zeros((8, COLS), F32)
@@ -193,8 +212,12 @@
 
     sx[8:24, :] = stiff_ref[...]
     qx[8:24, :] = react_ref[...]
-    for cp in first:
-        cp.wait()
+    drain(sxin, init_sem.at[0])
+    drain(sxin, init_sem.at[1])
+    sx[0:8, :] = sxin[0]
+    sx[24:32, :] = sxin[1]
+    qx[0:8, :] = sxin[2]
+    qx[24:32, :] = sxin[3]
     erow = lax.broadcasted_iota(jnp.int32, (32, COLS), 0) + (c_me * ROWS - 8)
     inside = jnp.logical_and(erow >= 0, erow < 128)
     st = jnp.where(inside, sx[...], 0.0)
@@ -242,7 +265,8 @@
     def ag_copy(k, idx, dz, dx, rows, dev):
         d = sidx(dz, dx, core)
         ref = xg.at[k, d] if rows is None else xg.at[k, d, :, rows]
-        return rdma(ref, ref, ag_send.at[k, idx], ag_recv.at[k, idx], dev)
+        which = {1: 0, 2: 1, 3: 2, 4: 3}.get(idx, 4 if 5 <= idx <= 10 else 5)
+        return rdma(ref, ref, ag_send.at[k], ag_recv.at[k, which], dev)
 
     def ag_copies(k):
         table = [
@@ -285,84 +309,76 @@
             s[f].start()
 
     def a2(u):
-        s = ag_copies(lax.rem(u, CHUNKS))
-        for i, z, f in ((5, 8, 15), (6, 9, 16), (7, 10, 17)):
-            s[i].wait_recv()
-            s[z].wait_recv()
+        k = lax.rem(u, CHUNKS)
+        s = ag_copies(k)
+        drain(xg.at[k, pl.ds(0, 3)], ag_recv.at[k, 4])
+        for f in (15, 16, 17):
             s[f].start()
 
     def a3(u):
-        s = ag_copies(lax.rem(u, CHUNKS))
-        for i in (0, 11, 12, 13, 14, 15, 16, 17):
-            s[i].wait_recv()
-        for cp in s:
-            cp.wait_send()
+        k = lax.rem(u, CHUNKS)
+        drain(xg.at[k, pl.ds(0, 8)], ag_recv.at[k, 5])
+        drain(xg.at[k, pl.ds(0, 15)], ag_send.at[k])
 
     frow = lax.broadcasted_iota(jnp.int32, (FB, COLS), 0)
     fold = frow == lax.broadcasted_iota(jnp.int32, (FB, COLS), 1) // SENS
 
-    def o_copies(u, k):
+    def o_copies(w):
+        n = lax.rem(w, 2)
         return [
             rdma(
-                oall.at[u, c_me], oall.at[u, c_me], o_send.at[k, j - 1], o_recv.at[u, j - 1],
+                oall.at[w, c_me], oall.at[w, c_me], o_send.at[n], o_recv.at[w],
                 {"cells": lax.rem(c_me + j, 8)},
             )
             for j in range(1, 8)
         ]
 
-    def observe(u):
-        k = lax.rem(u, CHUNKS)
-
-        for bb in range(CHUNK):
-
-            def dft(rp, carry, bb=bb):
-                x0 = xg[k, :, bb, 2 * rp].reshape(NT, COLS)
-                x1 = xg[k, :, bb, 2 * rp + 1].reshape(NT, COLS)
-                both = jnp.concatenate([x0, x1], axis=1)
-                v = jnp.dot(table_ref[...], both, preferred_element_type=F32).astype(BF16)
-                cols = pl.ds(pl.multiple_of(rp * 256, 256), 256)
-                spec[:, bb * 32 : bb * 32 + 32, cols] = v.reshape(GROUPS, 32, 256)
-                return carry
-
-            lax.fori_loop(0, ROWS // 2, dft, 0, unroll=8)
-
-        def group(g, carry):
+    def dft(u, sub):
+        k = lax.rem(u, CHUNKS)
+        for rp in range(ROWS // 2):
+            x0 = xg[k, :, 0, 2 * rp].reshape(NT, COLS)
+            x1 = xg[k, :, 0, 2 * rp + 1].reshape(NT, COLS)
+            both = jnp.concatenate([x0, x1], axis=1)
+            v = jnp.dot(table_ref[...], both, preferred_element_type=F32).astype(BF16)
+            spec[:, sub * 32 : sub * 32 + 32, rp * 256 : rp * 256 + 256] = v.reshape(GROUPS, 32, 256)
+
+    def observe(w, lo):
+        for g in range(lo, lo + GROUPS // 2):
             vg = spec[g]
             parts = []
             for p in range(2):
                 o = lax.dot_general(
                     vg, gv[p, g], (((1,), (1,)), ((), ())), preferred_element_type=F32
-                ).reshape(2 * CHUNK, FB, COLS)
+                ).reshape(2 * PASS, FB, COLS)
                 parts.append(jnp.sum(jnp.where(fold[None], o, 0.0), axis=1))
             a, b = parts
             rows = []
-            for bb in range(CHUNK):
-                rows.append(a[2 * bb : 2 * bb + 1] - b[2 * bb + 1 : 2 * bb + 2])
-                rows.append(a[2 * bb + 1 : 2 * bb + 2] + b[2 * bb : 2 * bb + 1])
-            oall[u, c_me, g] = jnp.concatenate(rows, axis=0)
-            return carry
-
-        lax.fori_loop(0, GROUPS, group, 0, unroll=4)
-        for cp in o_copies(u, k):
+            for n in range(PASS):
+                rows.append(a[2 * n : 2 * n + 1] - b[2 * n + 1 : 2 * n + 2])
+                rows.append(a[2 * n + 1 : 2 * n + 2] + b[2 * n : 2 * n + 1])
+            oall[w, c_me, g] = jnp.concatenate(rows, axis=0)
+
+    def oa(w):
+        observe(w, 0)
+
+    def ob(w):
+        observe(w, GROUPS // 2)
+        for cp in o_copies(w):
             cp.start()
 
     def sib_copy(k):
-        return rdma(y.at[k, other], rsib.at[k], sib_send.at[k], sib_recv.at[k], sib)
-
-    def pull(u):
-        k = lax.rem(u, CHUNKS)
-        for cp in o_copies(u, k):
-            cp.wait_recv()
-
-        def group(g, carry):
-            tot = oall[u, 0, g]
+        return rdma(y.at[k, other], rsib.at[k], rs_send.at[k], rs_recv.at[k, 0], sib)
+
+    def pull(w, lo):
+        for g in range(lo, lo + GROUPS // 2):
+            tot = oall[w, 0, g]
             for c in range(1, 8):
-                tot = tot + oall[u, c, g]
-            w = nwt[0 : 2 * CHUNK] * tot
+                tot = tot + oall[w, c, g]
+            wt = nwt[0 : 2 * PASS] * tot
             rows = []
-            for bb in range(CHUNK):
-                wr = jnp.broadcast_to(w[2 * bb : 2 * bb + 1], (FB, COLS))
-                wi = jnp.broadcast_to(w[2 * bb + 1 : 2 * bb + 2], (FB, COLS))
+            for n in range(PASS):
+                wr = jnp.broadcast_to(wt[2 * n : 2 * n + 1], (FB, COLS))
+                wi = jnp.broadcast_to(wt[2 * n + 1 : 2 * n + 2], (FB, COLS))
                 wr = jnp.where(fold, wr, 0.0)
                 wi = jnp.where(fold, wi, 0.0)
                 rows.append(jnp.concatenate([wr, wi], axis=1))
@@ -372,24 +388,27 @@
                 cols = slice(part * 512, part * 512 + 512)
                 gg = jnp.concatenate([gv[0, g, :, cols], gv[1, g, :, cols]], axis=0)
                 a = jnp.dot(wm, gg, preferred_element_type=F32).astype(BF16)
-                jr = pl.ds(pl.multiple_of(g * 32, 32), 32)
-                for bb in range(CHUNK):
-                    adj[bb, jr, cols] = a[bb * 32 : bb * 32 + 32]
-            return carry
-
-        lax.fori_loop(0, GROUPS, group, 0, unroll=4)
-        for bb in range(CHUNK):
-
-            def idft(rp, carry, bb=bb):
-                cols = pl.ds(pl.multiple_of(rp * 256, 256), 256)
-                v = jnp.dot(table_t_ref[...], adj[bb, :, cols], preferred_element_type=F32).astype(BF16)
-                for half in range(2):
-                    w = v[:, half * COLS : half * COLS + COLS].reshape(8, 2, STEPS, COLS)
-                    for c in range(2):
-                        y[k, c, :, bb, 2 * rp + half] = w[:, c]
-                return carry
-
-            lax.fori_loop(0, ROWS // 2, idft, 0, unroll=8)
+                for n in range(PASS):
+                    adj[n, g * 32 : g * 32 + 32, cols] = a[n * 32 : n * 32 + 32]
+
+    def pa(w):
+        drain(oall.at[w, pl.ds(0, 7)], o_recv.at[w])
+        pull(w, 0)
+
+    def pb(w):
+        pull(w, GROUPS // 2)
+        drain(oall.at[w, pl.ds(0, 7)], o_send.at[lax.rem(w, 2)])
+
+    def idft(u, sub):
+        k = lax.rem(u, CHUNKS)
+        for rp in range(ROWS // 2):
+            v = jnp.dot(
+                table_t_ref[...], adj[sub, :, rp * 256 : rp * 256 + 256], preferred_element_type=F32
+            ).astype(BF16)
+            for half in range(2):
+                part = v[:, half * COLS : half * COLS + COLS].reshape(8, 2, STEPS, COLS)
+                for c in range(2):
+                    y[k, c, :, 0, 2 * rp + half] = part[:, c]
         sib_copy(k).start()
 
     def block(zr, dx):
@@ -410,24 +429,24 @@
 
     def rzf_copy(k, dx):
         return rdma(
-            y.at[k, core, block(1, dx), :, FIRST], rzf.at[k, dx, :, FIRST], rzf_send.at[k, dx], rzf_recv.at[k, dx], zp
+            y.at[k, core, block(1, dx), :, FIRST], rzf.at[k, dx, :, FIRST], rs_send.at[k], rs_recv.at[k, dx or 5], zp
         )
 
     def rxg_copy(k, zr, dx):
         i = zr * 3 + dx - 1
         return rdma(
-            y.at[k, core, block(zr, dx), :, REST], rxg.at[k, i, :, REST], rxg_send.at[k, i], rxg_recv.at[k, i], xto[dx]
+            y.at[k, core, block(zr, dx), :, REST], rxg.at[k, i, :, REST], rs_send.at[k], rs_recv.at[k, 5 - zr], xto[dx]
         )
 
     def rxf_copy(k, dx):
         i = dx - 1
         return rdma(
-            y.at[k, core, block(0, dx), :, FIRST], rxf.at[k, i, :, FIRST], rxf_send.at[k, i], rxf_recv.at[k, i], xto[dx]
+            y.at[k, core, block(0, dx), :, FIRST], rxf.at[k, i, :, FIRST], rs_send.at[k], rs_recv.at[k, 5], xto[dx]
         )
 
     def rzg_copy(k):
         return rdma(
-            y.at[k, core, block(1, 0), :, REST], rzg.at[k, :, REST], rzg_send.at[k], rzg_recv.at[k], zp
+            y.at[k, core, block(1, 0), :, REST], rzg.at[k, :, REST], rs_send.at[k], rs_recv.at[k, 5], zp
         )
 
     def r1(u):
@@ -450,18 +469,13 @@
             rzf_copy(k, dx).wait_recv()
             add_rows(k, 0, dx, 0, SPLIT, (rzf.at[k, dx],))
             rxf_copy(k, dx).start()
-        for dx in (1, 3, 2):
-            rxg_copy(k, 1, dx).wait_recv()
+        drain(rxg.at[k, pl.ds(3, 3), :, REST], rs_recv.at[k, 4])
         add_rows(k, 1, 0, SPLIT, ROWS, [rxg.at[k, 3 + i] for i in range(3)])
         rzg_copy(k).start()
 
     def r3(u):
         k = lax.rem(u, CHUNKS)
-        rzf_copy(k, 0).wait_recv()
-        for dx in (1, 3, 2):
-            rxg_copy(k, 0, dx).wait_recv()
-            rxf_copy(k, dx).wait_recv()
-        rzg_copy(k).wait_recv()
+        drain(rxg.at[k, pl.ds(0, 4)], rs_recv.at[k, 5])
         for bb in range(CHUNK):
             b = k * CHUNK + bb
             for i in range(0, ROWS, 2):
@@ -480,18 +494,8 @@
                     r = rhs_ext[b, e] - (prior + m[n])
                     res_ext[b, e] = r
                     res_ref[b, i + n] = r
-        for cp in halo_copies(res_ext, k, halo_send.at[1], halo_recv.at[1]):
-            cp.start()
-        sib_copy(k).wait_send()
-        for dx in range(4):
-            rzf_copy(k, dx).wait_send()
-        for dx in (1, 2, 3):
-            rxf_copy(k, dx).wait_send()
-            for zr in range(2):
-                rxg_copy(k, zr, dx).wait_send()
-        rzg_copy(k).wait_send()
-        for cp in o_copies(u, k):
-            cp.wait_send()
+        halo_start(res_ext, 1, k)
+        drain(xg.at[k, pl.ds(0, 15)], rs_send.at[k])
 
     def own_to_gather(k):
         for bb in range(CHUNK):
@@ -504,22 +508,19 @@
             lax.fori_loop(0, ROWS // 4, body, 0, unroll=4)
 
     def begin(k):
-        for cp in halo_copies(rhs_ext, k, halo_send.at[0], halo_recv.at[0]):
-            cp.wait()
+        halo_finish(rhs_ext, 0, k)
         for bb in range(CHUNK):
             b = k * CHUNK + bb
             precondition(rhs_ext, b, 0)
 
     def update(k, mode):
-        for cp in halo_copies(res_ext, k, halo_send.at[1], halo_recv.at[1]):
-            cp.wait()
+        halo_finish(res_ext, 1, k)
 
         for bb in range(CHUNK):
             precondition(res_ext, k * CHUNK + bb, mode)
 
     def finish_map():
-        for cp in map_copies:
-            cp.wait()
+        drain(gv, loc_sem.at[6])
 
         def body(i, carry):
             rs = pl.ds(pl.multiple_of(lax.rem(i, 8) * 16, 16), 16)
@@ -542,35 +543,35 @@
         def _():
             update(lax.rem(u, CHUNKS), 2)
 
-    stages = {
-        "a0": a0, "a1": a1, "a2": a2, "a3": a3, "observe": observe, "pull": pull, "r1": r1, "r2": r2, "r3": r3
-    }
+    stages = {"a0": a0, "a1": a1, "a2": a2, "a3": a3, "r1": r1, "r2": r2, "r3": r3}
+    sampled = {"dft": dft, "idft": idft}
+    passes = {"oa": oa, "ob": ob, "pa": pa, "pb": pb}
 
     def step(t, carry):
-        for name, late in ORDER:
-            u = t - late
-            if name == "update":
-                advance(u)
-                continue
-
-            @pl.when(jnp.logical_and(u >= 0, u < JOBS))
-            def _(name=name, u=u):
-                stages[name](u)
-
-            if name == "a0":
-
-                @pl.when(t == 1)
-                def _():
-                    finish_map()
-
+        for name, sub, late in ORDER:
+            w = t - late
+
+            def run(name=name, sub=sub, w=w):
+                if name == "update":
+                    advance(w * PASS + sub)
+                elif name in stages:
+                    stages[name](w * PASS + sub)
+                elif name in sampled:
+                    sampled[name](w * PASS + sub, sub)
+                else:
+                    passes[name](w)
+
+            last = PASSES + PASSES // 2 if name == "update" else PASSES
+            pl.when(jnp.logical_and(w >= 0, w < last))(run)
+            if name == "a0" and sub == PASS - 1:
+                pl.when(t == 0)(finish_map)
         return carry
 
-    lax.fori_loop(0, JOBS + CHUNKS, step, 0)
+    lax.fori_loop(0, PASSES + PASSES // 2, step, 0)
 
 
 def shards(rhs, forward_map, stiffness, reaction, noise_weight, sensor_cell):
     table = transform_tables()
-    rhs_t = jnp.transpose(rhs, (1, 2, 0, 3))
     maps = forward_map.reshape(2, GROUPS, FB * SENS, CELLS)
     vm = pl.BlockSpec(memory_space=pltpu.VMEM)
     sm = pl.BlockSpec(memory_space=pltpu.SMEM)
@@ -581,20 +582,24 @@
     scratch = [
         pltpu.VMEM((2, GROUPS, FB * SENS, CELLS), BF16),
         pltpu.VMEM((CHUNKS, 16) + block, BF16),
-        pltpu.VMEM((GROUPS, 32 * CHUNK, CELLS), BF16),
-        pltpu.VMEM((CHUNK, NT, CELLS), BF16),
+        pltpu.VMEM((GROUPS, 32 * PASS, CELLS), BF16),
+        pltpu.VMEM((PASS, NT, CELLS), BF16),
         pltpu.VMEM((CHUNKS, 2, 8) + block, BF16),
         pltpu.VMEM((CHUNKS, 8) + block, BF16),
         pltpu.VMEM((CHUNKS, 4) + block, BF16),
         pltpu.VMEM((CHUNKS, 6) + block, BF16),
         pltpu.VMEM((CHUNKS, 3) + block, BF16),
         pltpu.VMEM((CHUNKS,) + block, BF16),
-        pltpu.VMEM((JOBS, 8, GROUPS, 2 * CHUNK, COLS), F32),
+        pltpu.VMEM((PASSES, 8, GROUPS, 2 * PASS, COLS), F32),
         pltpu.VMEM((6, EXT, STEPS, COLS), F32),
         pltpu.VMEM((6, EXT, STEPS, COLS), F32),
+        pltpu.VMEM((2, CHUNKS, 2, HALO, STEPS, COLS), BF16),
+        pltpu.VMEM((2, CHUNKS, 2, HALO, STEPS, COLS), BF16),
+        pltpu.VMEM((6, STEPS, ROWS, COLS), F32),
         pltpu.VMEM((6, ROWS + 2, STEPS, COLS), F32),
         pltpu.VMEM((32, COLS), F32),
         pltpu.VMEM((32, COLS), F32),
+        pltpu.VMEM((4, 8, COLS), F32),
         pltpu.VMEM((EXT, STEPS, COLS), F32),
         pltpu.VMEM((EXT, STEPS, COLS), F32),
         pltpu.VMEM((EXT, STEPS, COLS), F32),
@@ -602,25 +607,16 @@
         pltpu.VMEM((EXT, STEPS, COLS), F32),
         pltpu.VMEM((16, CELLS), BF16),
         pltpu.VMEM((8, COLS), F32),
-        dma((22,)),
-        dma((4,)),
-        dma((4,)),
-        dma((CHUNKS, 18)),
-        dma((CHUNKS, 18)),
+        dma((7,)),
+        dma((2,)),
         dma((CHUNKS,)),
+        dma((CHUNKS, 6)),
         dma((CHUNKS,)),
-        dma((CHUNKS, 4)),
-        dma((CHUNKS, 4)),
         dma((CHUNKS, 6)),
-        dma((CHUNKS, 6)),
-        dma((CHUNKS, 3)),
-        dma((CHUNKS, 3)),
-        dma((CHUNKS,)),
-        dma((CHUNKS,)),
-        dma((CHUNKS, 7)),
-        dma((JOBS, 7)),
-        dma((2, CHUNKS, 2)),
-        dma((2, CHUNKS, 2)),
+        dma((2,)),
+        dma((PASSES,)),
+        dma((2, CHUNKS)),
+        dma((2, CHUNKS)),
     ]
     sol, res = pl.pallas_call(
         kernel,
@@ -632,7 +628,7 @@
             collective_id=0, has_side_effects=True, vmem_limit_bytes=60 * 1024 * 1024
         ),
     )(
-        rhs_t,
+        rhs,
         maps,
         stiffness,
         reaction,

time: 174 us -> 150 us (0.86)
  Pallas kernels: 166 us -> 145 us
  local copies, waits for them, and re-layouts: 7.01 us -> 4.53 us
    pallas_call x1, Pallas kernels: 166 us -> 145 us  [shards(): pl.pallas_call(kernel, out_shape=(out, out), in_specs=[hb, hb, vm, vm, sm...]
    unnamed x3 -> x2, local copies, waits for them, and re-layouts: 7.01 us -> 4.53 us
where the time goes in v3:
time: 150 us
  Pallas kernels  145 us (97%)
  local copies, waits for them, and re-layouts  4.53 us (3%)
    pallas_call x1, Pallas kernels, shards(): pl.pallas_call(kernel, out_shape=(out, out), in_specs=[hb, hb, vm, vm, sm...  145 us
    unnamed x2, local copies, waits for them, and re-layouts  4.53 us

profile of v3, /device:TPU:0, one launch (start us, length us, event | category | flops | bytes accessed | tf_op | source)
XLA Modules:
  0.0 150.1 jit_solution(2738002972894215335)
XLA Ops:
  0.6 144.9 %shard_map.95 = (f32[6,16,16,128]{3,2,1,0:T(8,128)}, f32[6,16,16,128]{3,2,1,0:T(8,128)}) custom-call(f32[16,6,16,128]{3,2,1,0:T(8,128)} %rhs_hbm.1, bf16[2,8,128,2048]{3,2,1,0:T(8,128)(2,1)} %bitcast.3, f32[16,128]{1,0:T(8,128)} %stiff_ref.1, f32[16,128]{1,0:T(8,128)} %react_ref.1, f32[128]{0:T(128)} %weight_sm.1, s32[128]{0:T(128)} %cell_sm.1, ...), custom_call_target="tpu_custom_call" | custom-call | tf_op jit(solution)/shard_map/pallas_call | solution.py:621
  145.6 2.3 %copy.10 = f32[16,6,16,128]{3,2,1,0:T(8,128)} copy(f32[16,6,16,128]{3,0,2,1:T(8,128)} %bitcast.5) | data formatting | bytes 1572864
  147.9 2.3 %copy.11 = f32[16,6,16,128]{3,2,1,0:T(8,128)} copy(f32[16,6,16,128]{3,0,2,1:T(8,128)} %bitcast.4) | data formatting | bytes 1572864

commit v4 on v3

--- a/solution.py
+++ b/solution.py
@@ -232,6 +232,9 @@
     not_first = lane_s > 0
     not_last = lane_s < COLS - 1
 
+    def put_rows(ref, b, r, value):
+        ref.reshape(STEPS * 6 * ROWS, COLS)[pl.ds(b * ROWS + r, STEPS, stride=6 * ROWS), :] = value
+
     def sides(v):
         left = pltpu.roll(v, 1, 1)
         right = pltpu.roll(v, COLS - 1, 1)
@@ -258,7 +261,7 @@
                 elif mode == 1:
                     xf[b, q - 3] = xf[b, q - 3] + c_si[q] * new
                 elif HALO <= q < HALO + ROWS:
-                    sol_ref[b, q - HALO] = xf[b, q - 3] + c_si[q] * new
+                    put_rows(sol_ref, b, q - HALO, xf[b, q - 3] + c_si[q] * new)
 
     d_me = s_me
 
@@ -345,12 +348,12 @@
     def observe(w, lo):
         for g in range(lo, lo + GROUPS // 2):
             vg = spec[g]
+            both = jnp.concatenate([gv[0, g], gv[1, g]], axis=0)
+            o = lax.dot_general(vg, both, (((1,), (1,)), ((), ())), preferred_element_type=F32)
             parts = []
             for p in range(2):
-                o = lax.dot_general(
-                    vg, gv[p, g], (((1,), (1,)), ((), ())), preferred_element_type=F32
-                ).reshape(2 * PASS, FB, COLS)
-                parts.append(jnp.sum(jnp.where(fold[None], o, 0.0), axis=1))
+                op = o[:, p * COLS : p * COLS + COLS].reshape(2 * PASS, FB, COLS)
+                parts.append(jnp.sum(jnp.where(fold[None], op, 0.0), axis=1))
             a, b = parts
             rows = []
             for n in range(PASS):
@@ -493,7 +496,7 @@
                     prior = c_d[e] * xf[b, i + n + 1] - c_s[e] * nb
                     r = rhs_ext[b, e] - (prior + m[n])
                     res_ext[b, e] = r
-                    res_ref[b, i + n] = r
+                    put_rows(res_ref, b, i + n, r)
         halo_start(res_ext, 1, k)
         drain(xg.at[k, pl.ds(0, 15)], rs_send.at[k])
 
@@ -570,6 +573,17 @@
     lax.fori_loop(0, PASSES + PASSES // 2, step, 0)
 
 
+def write_out(a_ref, b_ref, a_out, b_out, sem):
+    copies = [
+        pltpu.make_async_copy(a_ref, a_out, sem.at[0]),
+        pltpu.make_async_copy(b_ref, b_out, sem.at[1]),
+    ]
+    for cp in copies:
+        cp.start()
+    for cp in copies:
+        cp.wait()
+
+
 def shards(rhs, forward_map, stiffness, reaction, noise_weight, sensor_cell):
     table = transform_tables()
     maps = forward_map.reshape(2, GROUPS, FB * SENS, CELLS)
@@ -578,7 +592,7 @@
     hb = pl.BlockSpec(memory_space=pl.ANY)
     block = (CHUNK, ROWS, STEPS, COLS)
     dma = pltpu.SemaphoreType.DMA
-    out = jax.ShapeDtypeStruct((6, ROWS, STEPS, COLS), F32)
+    out = jax.ShapeDtypeStruct((STEPS, 6, ROWS, COLS), F32)
     scratch = [
         pltpu.VMEM((2, GROUPS, FB * SENS, CELLS), BF16),
         pltpu.VMEM((CHUNKS, 16) + block, BF16),
@@ -637,7 +651,14 @@
         jnp.asarray(table, BF16),
         jnp.asarray(table.T, BF16),
     )
-    return (jnp.transpose(sol, (2, 0, 1, 3)), jnp.transpose(res, (2, 0, 1, 3)))
+    place = pl.BlockSpec(memory_space=pl.ANY)
+    return pl.pallas_call(
+        write_out,
+        out_shape=(out, out),
+        in_specs=[vm, vm],
+        out_specs=(place, place),
+        scratch_shapes=[dma((2,))],
+    )(sol, res)
 
 
 def solution(mesh):

time: 150 us -> 147 us (0.980)
  local copies, waits for them, and re-layouts: 4.53 us -> 0 us
    unnamed x2 -> x0, local copies, waits for them, and re-layouts: 4.53 us -> none
    pallas_call x0 -> x1, Pallas kernels: none -> 2.53 us  [shards(): pl.pallas_call(write_out, out_shape=(out, out), in_specs=[vm, vm], out_sp...]
where the time goes in v4:
time: 147 us
  Pallas kernels  146 us (99%)
    pallas_call x1, Pallas kernels, shards(): pl.pallas_call(kernel, out_shape=(out, out), in_specs=[hb, hb, vm, vm, sm...  144 us

profile of v4, /device:TPU:0, one launch (start us, length us, event | category | flops | bytes accessed | tf_op | source)
XLA Modules:
  0.0 146.8 jit_solution(4334023672120238467)
XLA Ops:
  0.6 143.6 %shard_map.95 = (f32[16,6,16,128]{3,2,1,0:T(8,128)}, f32[16,6,16,128]{3,2,1,0:T(8,128)}) custom-call(f32[16,6,16,128]{3,2,1,0:T(8,128)} %rhs_hbm.1, bf16[2,8,128,2048]{3,2,1,0:T(8,128)(2,1)} %bitcast.1, f32[16,128]{1,0:T(8,128)} %stiff_ref.1, f32[16,128]{1,0:T(8,128)} %react_ref.1, f32[128]{0:T(128)} %weight_sm.1, s32[128]{0:T(128)} %cell_sm.1, ...), custom_call_target="tpu_custom_call" | custom-call | tf_op jit(solution)/shard_map/pallas_call | solution.py:635
  144.2 2.5 %shard_map.96 = (f32[16,6,16,128]{3,2,1,0:T(8,128)}, f32[16,6,16,128]{3,2,1,0:T(8,128)}) custom-call(f32[16,6,16,128]{3,2,1,0:T(8,128)} %get-tuple-element.4.a_ref, f32[16,6,16,128]{3,2,1,0:T(8,128)} %get-tuple-element.5.b_ref), custom_call_target="tpu_custom_call" | custom-call | tf_op jit(solution)/shard_map/pallas_call | solution.py:655

commit v5 on v4

--- a/solution.py
+++ b/solution.py
@@ -28,6 +28,8 @@
 SPLIT = 8
 FIRST = pl.ds(0, SPLIT)
 REST = pl.ds(SPLIT, ROWS - SPLIT)
+LOW = pl.ds(SPLIT, 4)
+HIGH = pl.ds(SPLIT + 4, 4)
 PASS = 2
 PASSES = 12 // PASS
 ORDER = (
@@ -36,8 +38,8 @@
     ("a2", 0, 1),
     ("idft", 1, 2),
     ("r1", 0, 2),
+    ("a3", 0, 1),
     ("a2", 1, 1),
-    ("a3", 0, 1),
     ("dft", 0, 1),
     ("r1", 1, 2),
     ("a3", 1, 1),
@@ -78,8 +80,8 @@
     cell_sm,
     table_ref,
     table_t_ref,
-    sol_ref,
-    res_ref,
+    sol_out,
+    res_out,
     gv,
     xg,
     spec,
@@ -89,6 +91,7 @@
     rzf,
     rxg,
     rxf,
+    rel,
     rzg,
     oall,
     rhs_ext,
@@ -107,6 +110,9 @@
     c_d,
     marks,
     nwt,
+    sol_ref,
+    res_ref,
+    out_sem,
     loc_sem,
     init_sem,
     ag_send,
@@ -268,7 +274,7 @@
     def ag_copy(k, idx, dz, dx, rows, dev):
         d = sidx(dz, dx, core)
         ref = xg.at[k, d] if rows is None else xg.at[k, d, :, rows]
-        which = {1: 0, 2: 1, 3: 2, 4: 3}.get(idx, 4 if 5 <= idx <= 10 else 5)
+        which = {1: 0, 2: 1, 3: 2, 4: 3, 18: 6, 19: 6}.get(idx, 4 if 5 <= idx <= 10 else 5)
         return rdma(ref, ref, ag_send.at[k], ag_recv.at[k, which], dev)
 
     def ag_copies(k):
@@ -276,7 +282,7 @@
             (0, 0, None, sib),
             (0, 0, None, xp),
             (0, 0, None, xm),
-            (0, 0, None, xd),
+            (0, 0, FIRST, xd),
             (0, 0, None, zp),
             (1, 0, REST, xp),
             (1, 0, REST, xm),
@@ -291,6 +297,8 @@
             (1, 3, None, sib),
             (1, 1, None, sib),
             (1, 2, None, sib),
+            (0, 3, LOW, xp),
+            (0, 1, HIGH, xm),
         ]
         return [ag_copy(k, i, *row) for i, row in enumerate(table)]
 
@@ -306,14 +314,16 @@
         s[4].wait_recv()
         for i in (5, 6, 7, 14):
             s[i].start()
-        for i, z, f in ((1, 8, 11), (2, 9, 12), (3, 10, 13)):
+        for i, more in ((1, (18, 8, 11)), (2, (19, 9, 12)), (3, (10,))):
             s[i].wait_recv()
-            s[z].start()
-            s[f].start()
+            for n in more:
+                s[n].start()
 
     def a2(u):
         k = lax.rem(u, CHUNKS)
         s = ag_copies(k)
+        drain(xg.at[k, 0, :, REST], ag_recv.at[k, 6])
+        s[13].start()
         drain(xg.at[k, pl.ds(0, 3)], ag_recv.at[k, 4])
         for f in (15, 16, 17):
             s[f].start()
@@ -449,12 +459,21 @@
 
     def rzg_copy(k):
         return rdma(
-            y.at[k, core, block(1, 0), :, REST], rzg.at[k, :, REST], rs_send.at[k], rs_recv.at[k, 5], zp
+            y.at[k, core, block(1, 0), :, REST], rzg.at[k, :, REST], rs_send.at[k], rs_recv.at[k, 7], zp
         )
+
+    def rel_copies(k):
+        return [
+            rdma(y.at[k, core, block(0, 2), :, rows], rel.at[k, n, :, rows], rs_send.at[k], rs_recv.at[k, 6], dev)
+            for n, rows, dev in ((0, LOW, xp), (1, HIGH, xm))
+        ]
 
     def r1(u):
         k = lax.rem(u, CHUNKS)
         sib_copy(k).wait_recv()
+        add_rows(k, 0, 2, SPLIT, ROWS, ())
+        for cp in rel_copies(k):
+            cp.start()
         for dx in (2, 1, 3):
             add_rows(k, 1, dx, 0, SPLIT, ())
             rzf_copy(k, dx).start()
@@ -462,9 +481,6 @@
             rxg_copy(k, 1, dx).start()
         add_rows(k, 1, 0, 0, SPLIT, ())
         rzf_copy(k, 0).start()
-        for dx in (2, 1, 3):
-            add_rows(k, 0, dx, SPLIT, ROWS, ())
-            rxg_copy(k, 0, dx).start()
 
     def r2(u):
         k = lax.rem(u, CHUNKS)
@@ -475,10 +491,19 @@
         drain(rxg.at[k, pl.ds(3, 3), :, REST], rs_recv.at[k, 4])
         add_rows(k, 1, 0, SPLIT, ROWS, [rxg.at[k, 3 + i] for i in range(3)])
         rzg_copy(k).start()
+        drain(rel.at[k, 0, :, REST], rs_recv.at[k, 6])
+        mid = SPLIT + 4
+        add_rows(k, 0, 1, SPLIT, mid, (rel.at[k, 0],))
+        add_rows(k, 0, 1, mid, ROWS, ())
+        rxg_copy(k, 0, 1).start()
+        add_rows(k, 0, 3, SPLIT, mid, ())
+        add_rows(k, 0, 3, mid, ROWS, (rel.at[k, 1],))
+        rxg_copy(k, 0, 3).start()
 
     def r3(u):
         k = lax.rem(u, CHUNKS)
-        drain(rxg.at[k, pl.ds(0, 4)], rs_recv.at[k, 5])
+        drain(rxg.at[k, pl.ds(0, 3)], rs_recv.at[k, 5])
+        rzg_copy(k).wait_recv()
         for bb in range(CHUNK):
             b = k * CHUNK + bb
             for i in range(0, ROWS, 2):
@@ -488,7 +513,7 @@
                 if i < SPLIT:
                     arrived = [rzf.at[k, 0]] + [rxf.at[k, n] for n in range(3)]
                 else:
-                    arrived = [rzg.at[k]] + [rxg.at[k, n] for n in range(3)]
+                    arrived = [rzg.at[k]] + [rxg.at[k, n] for n in (0, 2)]
                 m = total(k, 0, 0, bb, rs, arrived)
                 for n in range(2):
                     e = HALO + i + n
@@ -498,6 +523,11 @@
                     res_ext[b, e] = r
                     put_rows(res_ref, b, i + n, r)
         halo_start(res_ext, 1, k)
+
+        @pl.when(u >= CHUNKS)
+        def _():
+            pltpu.make_async_copy(res_ref.at[:, k], res_out.at[:, k], out_sem.at[1]).start()
+
         drain(xg.at[k, pl.ds(0, 15)], rs_send.at[k])
 
     def own_to_gather(k):
@@ -521,6 +551,8 @@
 
         for bb in range(CHUNK):
             precondition(res_ext, k * CHUNK + bb, mode)
+        if mode == 2:
+            pltpu.make_async_copy(sol_ref.at[:, k], sol_out.at[:, k], out_sem.at[0]).start()
 
     def finish_map():
         drain(gv, loc_sem.at[6])
@@ -571,6 +603,8 @@
         return carry
 
     lax.fori_loop(0, PASSES + PASSES // 2, step, 0)
+    drain(sol_ref, out_sem.at[0])
+    drain(res_ref, out_sem.at[1])
 
 
 def write_out(a_ref, b_ref, a_out, b_out, sem):
@@ -603,6 +637,7 @@
         pltpu.VMEM((CHUNKS, 4) + block, BF16),
         pltpu.VMEM((CHUNKS, 6) + block, BF16),
         pltpu.VMEM((CHUNKS, 3) + block, BF16),
+        pltpu.VMEM((CHUNKS, 2) + block, BF16),
         pltpu.VMEM((CHUNKS,) + block, BF16),
         pltpu.VMEM((PASSES, 8, GROUPS, 2 * PASS, COLS), F32),
         pltpu.VMEM((6, EXT, STEPS, COLS), F32),
@@ -621,12 +656,15 @@
         pltpu.VMEM((EXT, STEPS, COLS), F32),
         pltpu.VMEM((16, CELLS), BF16),
         pltpu.VMEM((8, COLS), F32),
+        pltpu.VMEM((STEPS, 6, ROWS, COLS), F32),
+        pltpu.VMEM((STEPS, 6, ROWS, COLS), F32),
+        dma((2,)),
         dma((7,)),
         dma((2,)),
         dma((CHUNKS,)),
-        dma((CHUNKS, 6)),
+        dma((CHUNKS, 7)),
         dma((CHUNKS,)),
-        dma((CHUNKS, 6)),
+        dma((CHUNKS, 8)),
         dma((2,)),
         dma((PASSES,)),
         dma((2, CHUNKS)),
@@ -636,7 +674,7 @@
         kernel,
         out_shape=(out, out),
         in_specs=[hb, hb, vm, vm, sm, sm, vm, vm],
-        out_specs=(vm, vm),
+        out_specs=(hb, hb),
         scratch_shapes=scratch,
         compiler_params=pltpu.CompilerParams(
             collective_id=0, has_side_effects=True, vmem_limit_bytes=60 * 1024 * 1024

time: 147 us -> 143 us (0.973)
  Pallas kernels: 146 us -> 143 us
    pallas_call x1, Pallas kernels: 144 us -> 140 us  [shards(): pl.pallas_call(kernel, out_shape=(out, out), in_specs=[hb, hb, vm, vm, sm...]
where the time goes in v5:
time: 143 us
  Pallas kernels  143 us (100%)
    pallas_call x1, Pallas kernels, shards(): pl.pallas_call(kernel, out_shape=(out, out), in_specs=[hb, hb, vm, vm, sm...  140 us

profile of v5, /device:TPU:0, one launch (start us, length us, event | category | flops | bytes accessed | tf_op | source)
XLA Modules:
  0.0 143.3 jit_solution(12014054303176800465)
XLA Ops:
  0.6 140.2 %shard_map.95 = (f32[16,6,16,128]{3,2,1,0:T(8,128)}, f32[16,6,16,128]{3,2,1,0:T(8,128)}) custom-call(f32[16,6,16,128]{3,2,1,0:T(8,128)} %rhs_hbm.1, bf16[2,8,128,2048]{3,2,1,0:T(8,128)(2,1)} %bitcast.1, f32[16,128]{1,0:T(8,128)} %stiff_ref.1, f32[16,128]{1,0:T(8,128)} %react_ref.1, f32[128]{0:T(128)} %weight_sm.1, s32[128]{0:T(128)} %cell_sm.1, ...), custom_call_target="tpu_custom_call" | custom-call | tf_op jit(solution)/shard_map/pallas_call | solution.py:673
  140.8 2.5 %shard_map.96 = (f32[16,6,16,128]{3,2,1,0:T(8,128)}, f32[16,6,16,128]{3,2,1,0:T(8,128)}) custom-call(f32[16,6,16,128]{3,2,1,0:T(8,128)} %get-tuple-element.4.a_ref, f32[16,6,16,128]{3,2,1,0:T(8,128)} %get-tuple-element.5.b_ref), custom_call_target="tpu_custom_call" | custom-call | tf_op jit(solution)/shard_map/pallas_call | solution.py:693

commit v6 on v5

--- a/solution.py
+++ b/solution.py
@@ -53,8 +53,8 @@
     ("a1", 0, 0),
     ("r3", 0, 2),
     ("pa", 0, 1),
+    ("a1", 1, 0),
     ("pb", 0, 1),
-    ("a1", 1, 0),
     ("idft", 0, 1),
     ("r3", 1, 2),
 )
@@ -172,7 +172,6 @@
     peers = [sib, xp, xm, xd, zp] + [{"cells": lax.rem(c_me + j, 8)} for j in range(1, 8)]
     for peer in peers:
         pl.semaphore_signal(barrier, inc=1, device_id=peer, device_id_type=MESH)
-    pl.semaphore_wait(barrier, len(peers))
 
     def coef_copies():
         return [
@@ -193,15 +192,11 @@
         for n, lo in ((0, 0), (1, HALO + ROWS)):
             ref[k, pl.ds(lo, HALO)] = hin[phase, k, n].astype(F32)
 
-    first = coef_copies()
-    for cp in first:
-        cp.start()
     for b in range(6):
         rhs_copies[b].wait()
         flat = stage.at[b].reshape(STEPS * ROWS, COLS)
         for r in range(ROWS):
             rhs_ext[b, HALO + r] = flat[pl.ds(r, STEPS, stride=ROWS), :]
-        halo_start(rhs_ext, 0, b)
 
     lane = lax.broadcasted_iota(jnp.int32, (8, COLS), 1)
     acc = jnp.zeros((8, COLS), F32)
@@ -215,6 +210,12 @@
     for part in range(4):
         cell_id = lax.broadcasted_iota(jnp.int32, (16, 512), 1) + (c_me * CELLS + part * 512)
         marks[:, part * 512 : (part + 1) * 512] = jnp.where(cell_id == target, 1.0, 0.0).astype(BF16)
+
+    pl.semaphore_wait(barrier, len(peers))
+    for cp in coef_copies():
+        cp.start()
+    for b in range(6):
+        halo_start(rhs_ext, 0, b)
 
     sx[8:24, :] = stiff_ref[...]
     qx[8:24, :] = react_ref[...]

time: 143 us -> 143 us (level)
  no operation moved by 1% of the time
where the time goes in v6:
time: 143 us
  Pallas kernels  142 us (99%)
    pallas_call x1, Pallas kernels, shards(): pl.pallas_call(kernel, out_shape=(out, out), in_specs=[hb, hb, vm, vm, sm...  139 us

profile of v6, /device:TPU:0, one launch (start us, length us, event | category | flops | bytes accessed | tf_op | source)
XLA Modules:
  0.0 142.6 jit_solution(8062135605130074878)
XLA Ops:
  0.6 139.5 %shard_map.95 = (f32[16,6,16,128]{3,2,1,0:T(8,128)}, f32[16,6,16,128]{3,2,1,0:T(8,128)}) custom-call(f32[16,6,16,128]{3,2,1,0:T(8,128)} %rhs_hbm.1, bf16[2,8,128,2048]{3,2,1,0:T(8,128)(2,1)} %bitcast.1, f32[16,128]{1,0:T(8,128)} %stiff_ref.1, f32[16,128]{1,0:T(8,128)} %react_ref.1, f32[128]{0:T(128)} %weight_sm.1, s32[128]{0:T(128)} %cell_sm.1, ...), custom_call_target="tpu_custom_call" | custom-call | tf_op jit(solution)/shard_map/pallas_call | solution.py:674
  140.1 2.5 %shard_map.96 = (f32[16,6,16,128]{3,2,1,0:T(8,128)}, f32[16,6,16,128]{3,2,1,0:T(8,128)}) custom-call(f32[16,6,16,128]{3,2,1,0:T(8,128)} %get-tuple-element.4.a_ref, f32[16,6,16,128]{3,2,1,0:T(8,128)} %get-tuple-element.5.b_ref), custom_call_target="tpu_custom_call" | custom-call | tf_op jit(solution)/shard_map/pallas_call | solution.py:694
